TPU v7x, 32 devices: a whole 2x2x4 slice. The times are simulated.
32 devices in a mesh: dp: 8 (over y, x, core), ctx: 4 (over z).
Axes of the slice: x: 2, y: 2, z: 4, core: 2. Of those that a mesh axis runs over, the one named last changes fastest.
Arguments:
- tokens: bfloat16 [16, 1024, 768], P('dp', 'ctx'), may hold values from -6 to 6
- segments: int32 [16, 1024], P('dp', 'ctx'), may hold values from 0 to 16, as said below
- positions: int32 [16, 1024], P('dp', 'ctx'), may hold values from 0 to 799, as said below
- qkv_weight: bfloat16 [1769472], P(('dp', 'ctx')), may hold values from -0.21875 to 0.21875
- out_weight: bfloat16 [589824], P(('dp', 'ctx')), may hold values from -1.75 to 1.75
- gate_up_weight: bfloat16 [4718592], P(('dp', 'ctx')), may hold values from -0.21875 to 0.21875
- down_weight: bfloat16 [2359296], P(('dp', 'ctx')), may hold values from -0.109375 to 0.109375
- first_gain: bfloat16 [768], P(('dp', 'ctx')), may hold values from 0.099609375 to 1.8984375
- first_bias: bfloat16 [768], P(('dp', 'ctx')), may hold values from -3 to 3
- second_gain: bfloat16 [768], P(('dp', 'ctx')), may hold values from 0.099609375 to 1.8984375
- second_bias: bfloat16 [768], P(('dp', 'ctx')), may hold values from -3 to 3
- output_grad: bfloat16 [16, 1024, 768], P('dp', 'ctx'), may hold values from -6 to 6
Outputs:
- output: bfloat16 [16, 1024, 768], P('dp', 'ctx')
- input_grad: float32 [16, 1024, 768], P('dp', 'ctx')
- qkv_weight_grad: float32 [1769472], P(('dp', 'ctx'))
- out_weight_grad: float32 [589824], P(('dp', 'ctx'))
- gate_up_weight_grad: float32 [4718592], P(('dp', 'ctx'))
- down_weight_grad: float32 [2359296], P(('dp', 'ctx'))
- first_gain_grad: float32 [768], P(('dp', 'ctx'))
- first_bias_grad: float32 [768], P(('dp', 'ctx'))
- second_gain_grad: float32 [768], P(('dp', 'ctx'))
- second_bias_grad: float32 [768], P(('dp', 'ctx'))
Inputs may be any that keep to these rules, and one draw needn't show every extreme that they name: `segments`: each sequence is packed with whole documents of 60 to 800 tokens; a document's tokens carry one id, ids count up from 0 along the sequence; every draw holds a document of exactly 800 tokens and a sequence with the most documents. `positions`: each token's place within its document, counting from 0 at the document's first token.
All inputs are finite; a program needn't handle non-finite values.
Results may differ from a plain program's by a relative error of at most 0.015.
Values may be sent and summed in bfloat16 or wider, within the bound.
No kernel may reach another device: no remote copies, remote signals or barrier semaphores. Data moves between devices by JAX's collectives and lax.ppermute only.
A program may use at most 192 MiB of HBM per device.

v0:
```python
import math

import jax
import jax.numpy as jnp
from jax import lax
from jax.sharding import PartitionSpec as P

D = 768
HEADS = 12
HEAD_DIM = 64
FF = 3072


norm_epsilon = 1e-05
rotary_base = 1000.0
masked_score = -1000000000.0


def rotary_tables(positions, head_size):
    half_dim = head_size // 2
    counter = jnp.arange(half_dim, dtype=jnp.float32)
    inverse = jnp.exp(counter * (-2.0 * math.log(rotary_base) / head_size))
    angles = positions.astype(jnp.float32)[..., None] * inverse
    return (jnp.cos(angles)[..., None, :], jnp.sin(angles)[..., None, :])


def rotate(values, cosine_table, sine_table):
    half_dim = values.shape[-1] // 2
    first_half = values[..., :half_dim]
    second_half = values[..., half_dim:]
    return jnp.concatenate(
        [
            first_half * cosine_table - second_half * sine_table,
            second_half * cosine_table + first_half * sine_table,
        ],
        axis=-1,
    )


def rotate_back(grads, cosine_table, sine_table):
    half_dim = grads.shape[-1] // 2
    first_half = grads[..., :half_dim]
    second_half = grads[..., half_dim:]
    return jnp.concatenate(
        [
            first_half * cosine_table + second_half * sine_table,
            second_half * cosine_table - first_half * sine_table,
        ],
        axis=-1,
    )


def layer_norm(hidden_sum, gain, bias):
    average = jnp.mean(hidden_sum, axis=-1, keepdims=True)
    centered = hidden_sum - average
    variance = jnp.mean(centered * centered, axis=-1, keepdims=True)
    reciprocal = lax.rsqrt(variance + norm_epsilon)
    normed = centered * reciprocal
    return (normed * gain + bias, normed, reciprocal)


def norm_back(upstream, normed, reciprocal, gain):
    gain_grad = jnp.sum(upstream * normed, axis=0)
    bias_grad = jnp.sum(upstream, axis=0)
    normed_grad = upstream * gain
    input_part = reciprocal * (
        normed_grad
        - jnp.mean(normed_grad, axis=-1, keepdims=True)
        - normed * jnp.mean(normed_grad * normed, axis=-1, keepdims=True)
    )
    return (input_part, gain_grad, bias_grad)


def contract_rows(left, right):
    return lax.dot_general(
        left, right, (((0,), (0,)), ((), ())), preferred_element_type=jnp.float32
    )


def back_dot(left, right):
    return lax.dot_general(
        left, right, (((1,), (1,)), ((), ())), preferred_element_type=jnp.float32
    )


def unpack(gathered):
    qkv_flat, out_flat, gate_up_flat, down_flat, gain_one, bias_one, gain_two, bias_two = gathered
    return (
        qkv_flat.reshape(D, 3 * D),
        out_flat.reshape(D, D),
        gate_up_flat.reshape(D, 2 * FF),
        down_flat.reshape(FF, D),
        gain_one.astype(jnp.float32),
        bias_one.astype(jnp.float32),
        gain_two.astype(jnp.float32),
        bias_two.astype(jnp.float32),
    )


def head_slice(array, offset, lanes):
    piece = lax.dynamic_slice_in_dim(array, offset, lanes, 2)
    return piece.reshape(array.shape[0], array.shape[1], 2, HEAD_DIM)


def pair_logits(query_pair, key_pair, same_doc):
    scores = jnp.einsum("sqhd,skhd->shqk", query_pair, key_pair, preferred_element_type=jnp.float32)
    return jnp.where(same_doc, scores * 0.125, masked_score)


def attend(queries, keys_all, values_all, same_doc):
    seq_count, row_count, feature_count = queries.shape
    lanes = 2 * HEAD_DIM

    def pair_step(head_pair, buffers):
        out_buffer, total_buffer = buffers
        offset = head_pair * lanes
        logits = pair_logits(
            head_slice(queries, offset, lanes), head_slice(keys_all, offset, lanes), same_doc
        )
        highest = jnp.max(logits, axis=-1, keepdims=True)
        log_total = highest + jnp.log(jnp.sum(jnp.exp(logits - highest), axis=-1, keepdims=True))
        probs_low = jnp.exp(logits - log_total).astype(jnp.bfloat16)
        attended = jnp.einsum(
            "shqk,skhd->sqhd",
            probs_low,
            head_slice(values_all, offset, lanes),
            preferred_element_type=jnp.float32,
        ).astype(jnp.bfloat16)
        out_buffer = lax.dynamic_update_slice_in_dim(
            out_buffer, attended.reshape(seq_count, row_count, lanes), offset, 2
        )
        total_buffer = lax.dynamic_update_slice_in_dim(
            total_buffer, log_total[..., 0], 2 * head_pair, 1
        )
        return (out_buffer, total_buffer)

    initial = (
        jnp.zeros((seq_count, row_count, feature_count), jnp.bfloat16),
        jnp.zeros((seq_count, HEADS, row_count), jnp.float32),
    )
    return lax.fori_loop(0, HEADS // 2, pair_step, initial)


def attend_back(queries, keys_all, values_all, same_doc, total_buffer, attended_grad):
    seq_count, row_count, feature_count = queries.shape
    key_count = keys_all.shape[1]
    lanes = 2 * HEAD_DIM

    def pair_step(head_pair, buffers):
        query_buffer, key_buffer, value_buffer = buffers
        offset = head_pair * lanes
        query_pair = head_slice(queries, offset, lanes)
        key_pair = head_slice(keys_all, offset, lanes)
        value_pair = head_slice(values_all, offset, lanes)
        grad_pair = head_slice(attended_grad, offset, lanes)
        logits = pair_logits(query_pair, key_pair, same_doc)
        log_total = lax.dynamic_slice_in_dim(total_buffer, 2 * head_pair, 2, 1)
        probs = jnp.exp(logits - log_total[..., None])
        prob_grad = jnp.einsum(
            "sqhd,skhd->shqk", grad_pair, value_pair, preferred_element_type=jnp.float32
        )
        logit_grad = probs * (prob_grad - jnp.sum(probs * prob_grad, axis=-1, keepdims=True))
        score_grad = (logit_grad * 0.125).astype(jnp.bfloat16)
        query_part = jnp.einsum(
            "shqk,skhd->sqhd", score_grad, key_pair, preferred_element_type=jnp.float32
        )
        key_part = jnp.einsum(
            "shqk,sqhd->skhd", score_grad, query_pair, preferred_element_type=jnp.float32
        )
        value_part = jnp.einsum(
            "shqk,sqhd->skhd",
            probs.astype(jnp.bfloat16),
            grad_pair,
            preferred_element_type=jnp.float32,
        )
        query_buffer = lax.dynamic_update_slice_in_dim(
            query_buffer, query_part.reshape(seq_count, row_count, lanes), offset, 2
        )
        key_buffer = lax.dynamic_update_slice_in_dim(
            key_buffer, key_part.reshape(seq_count, key_count, lanes), offset, 2
        )
        value_buffer = lax.dynamic_update_slice_in_dim(
            value_buffer, value_part.reshape(seq_count, key_count, lanes), offset, 2
        )
        return (query_buffer, key_buffer, value_buffer)

    initial = (
        jnp.zeros((seq_count, row_count, feature_count), jnp.float32),
        jnp.zeros((seq_count, key_count, feature_count), jnp.float32),
        jnp.zeros((seq_count, key_count, feature_count), jnp.float32),
    )
    return lax.fori_loop(0, HEADS // 2, pair_step, initial)


def local(
    tokens,
    segments,
    positions,
    qkv_weight,
    out_weight,
    gate_up_weight,
    down_weight,
    first_gain,
    first_bias,
    second_gain,
    second_bias,
    output_grad,
):
    seq_count = tokens.shape[0]
    row_count = tokens.shape[1]
    gathered = (
        lax.all_gather(qkv_weight, ("dp", "ctx"), axis=0, tiled=True),
        lax.all_gather(out_weight, ("dp", "ctx"), axis=0, tiled=True),
        lax.all_gather(gate_up_weight, ("dp", "ctx"), axis=0, tiled=True),
        lax.all_gather(down_weight, ("dp", "ctx"), axis=0, tiled=True),
        lax.all_gather(first_gain, ("dp", "ctx"), axis=0, tiled=True),
        lax.all_gather(first_bias, ("dp", "ctx"), axis=0, tiled=True),
        lax.all_gather(second_gain, ("dp", "ctx"), axis=0, tiled=True),
        lax.all_gather(second_bias, ("dp", "ctx"), axis=0, tiled=True),
    )
    qkv_mat, out_mat, gate_up_mat, down_mat, gain_one, bias_one, gain_two, bias_two = unpack(
        gathered
    )
    token_rows = tokens.reshape(seq_count * row_count, D)
    cosine_table, sine_table = rotary_tables(positions, HEAD_DIM)
    projected = jnp.dot(token_rows, qkv_mat, preferred_element_type=jnp.float32)
    projected = projected.reshape(seq_count, row_count, 3, HEADS, HEAD_DIM)
    queries = (
        rotate(projected[:, :, 0], cosine_table, sine_table)
        .astype(jnp.bfloat16)
        .reshape(seq_count, row_count, D)
    )
    keys_low = (
        rotate(projected[:, :, 1], cosine_table, sine_table)
        .astype(jnp.bfloat16)
        .reshape(seq_count, row_count, D)
    )
    values_low = projected[:, :, 2].astype(jnp.bfloat16).reshape(seq_count, row_count, D)
    key_ids = segments.astype(jnp.bfloat16)
    keys_all, values_all, ids_all = (
        lax.all_gather(keys_low, "ctx", axis=1, tiled=True),
        lax.all_gather(values_low, "ctx", axis=1, tiled=True),
        lax.all_gather(key_ids, "ctx", axis=1, tiled=True),
    )
    same_doc = (
        segments.astype(jnp.float32)[:, None, :, None]
        == ids_all.astype(jnp.float32)[:, None, None, :]
    )
    attended, total_buffer = attend(queries, keys_all, values_all, same_doc)
    attended_rows = attended.reshape(seq_count * row_count, D)
    branch = jnp.dot(attended_rows, out_mat, preferred_element_type=jnp.float32)
    normed_one, hat_one, recip_one = layer_norm(
        token_rows.astype(jnp.float32) + branch, gain_one, bias_one
    )
    normed_low = normed_one.astype(jnp.bfloat16)
    gate_up = jnp.dot(normed_low, gate_up_mat, preferred_element_type=jnp.float32)
    gate_part = gate_up[:, :FF]
    up_part = gate_up[:, FF:]
    sigmoid_gate = jax.nn.sigmoid(gate_part)
    silu_gate = gate_part * sigmoid_gate
    hidden = (silu_gate * up_part).astype(jnp.bfloat16)
    mlp_out = jnp.dot(hidden, down_mat, preferred_element_type=jnp.float32)
    result, hat_two, recip_two = layer_norm(normed_one + mlp_out, gain_two, bias_two)
    output = result.astype(jnp.bfloat16).reshape(tokens.shape)
    again = (
        lax.all_gather(qkv_weight, ("dp", "ctx"), axis=0, tiled=True),
        lax.all_gather(out_weight, ("dp", "ctx"), axis=0, tiled=True),
        lax.all_gather(gate_up_weight, ("dp", "ctx"), axis=0, tiled=True),
        lax.all_gather(down_weight, ("dp", "ctx"), axis=0, tiled=True),
        lax.all_gather(first_gain, ("dp", "ctx"), axis=0, tiled=True),
        lax.all_gather(first_bias, ("dp", "ctx"), axis=0, tiled=True),
        lax.all_gather(second_gain, ("dp", "ctx"), axis=0, tiled=True),
        lax.all_gather(second_bias, ("dp", "ctx"), axis=0, tiled=True),
    )
    qkv_mat, out_mat, gate_up_mat, down_mat, gain_one, bias_one, gain_two, bias_two = unpack(again)
    keys_all, values_all, ids_all = (
        lax.all_gather(keys_low, "ctx", axis=1, tiled=True),
        lax.all_gather(values_low, "ctx", axis=1, tiled=True),
        lax.all_gather(key_ids, "ctx", axis=1, tiled=True),
    )
    upstream = output_grad.reshape(seq_count * row_count, D).astype(jnp.float32)
    second_grad, second_gain_part, second_bias_part = norm_back(
        upstream, hat_two, recip_two, gain_two
    )
    mlp_grad = second_grad.astype(jnp.bfloat16)
    down_part = contract_rows(hidden, mlp_grad)
    hidden_grad = back_dot(mlp_grad, down_mat)
    gate_grad = hidden_grad * up_part * (sigmoid_gate * (1.0 + gate_part * (1.0 - sigmoid_gate)))
    up_grad = hidden_grad * silu_gate
    gate_up_grad = jnp.concatenate([gate_grad, up_grad], axis=1).astype(jnp.bfloat16)
    gate_up_part = contract_rows(normed_low, gate_up_grad)
    gate_up_flat = gate_up_part.reshape(-1)
    early = (
        lax.psum_scatter(gate_up_flat, ("dp", "ctx"), scatter_dimension=0, tiled=True),
        lax.psum_scatter(second_gain_part, ("dp", "ctx"), scatter_dimension=0, tiled=True),
        lax.psum_scatter(second_bias_part, ("dp", "ctx"), scatter_dimension=0, tiled=True),
    )
    gate_up_share, gain_two_share, bias_two_share = early
    normed_grad = second_grad + back_dot(gate_up_grad, gate_up_mat)
    first_grad, first_gain_part, first_bias_part = norm_back(
        normed_grad, hat_one, recip_one, gain_one
    )
    branch_grad = first_grad.astype(jnp.bfloat16)
    out_part = contract_rows(attended_rows, branch_grad)
    attended_grad = (
        back_dot(branch_grad, out_mat).astype(jnp.bfloat16).reshape(seq_count, row_count, D)
    )
    query_grad, key_partial, value_partial = attend_back(
        queries, keys_all, values_all, same_doc, total_buffer, attended_grad
    )
    key_grad, value_grad = (
        lax.psum_scatter(
            key_partial.astype(jnp.bfloat16), "ctx", scatter_dimension=1, tiled=True
        ).astype(jnp.float32),
        lax.psum_scatter(
            value_partial.astype(jnp.bfloat16), "ctx", scatter_dimension=1, tiled=True
        ).astype(jnp.float32),
    )
    head_shape = (seq_count, row_count, HEADS, HEAD_DIM)
    query_raw = rotate_back(query_grad.reshape(head_shape), cosine_table, sine_table).reshape(-1, D)
    key_raw = rotate_back(key_grad.reshape(head_shape), cosine_table, sine_table).reshape(-1, D)
    projected_grad = jnp.concatenate(
        [query_raw, key_raw, value_grad.reshape(-1, D)], axis=1
    ).astype(jnp.bfloat16)
    qkv_part = contract_rows(token_rows, projected_grad)
    input_grad = (back_dot(projected_grad, qkv_mat) + first_grad).reshape(tokens.shape)
    qkv_flat = qkv_part.reshape(-1)
    out_flat = out_part.reshape(-1)
    down_flat = down_part.reshape(-1)
    late = (
        lax.psum_scatter(qkv_flat, ("dp", "ctx"), scatter_dimension=0, tiled=True),
        lax.psum_scatter(out_flat, ("dp", "ctx"), scatter_dimension=0, tiled=True),
        lax.psum_scatter(down_flat, ("dp", "ctx"), scatter_dimension=0, tiled=True),
        lax.psum_scatter(first_gain_part, ("dp", "ctx"), scatter_dimension=0, tiled=True),
        lax.psum_scatter(first_bias_part, ("dp", "ctx"), scatter_dimension=0, tiled=True),
    )
    qkv_share, out_share, down_share, gain_one_share, bias_one_share = late
    return (
        output,
        input_grad,
        qkv_share,
        out_share,
        gate_up_share,
        down_share,
        gain_one_share,
        bias_one_share,
        gain_two_share,
        bias_two_share,
    )


def solution(mesh):
    in_specs = (
        P("dp", "ctx", None),
        P("dp", "ctx"),
        P("dp", "ctx"),
        P(("dp", "ctx")),
        P(("dp", "ctx")),
        P(("dp", "ctx")),
        P(("dp", "ctx")),
        P(("dp", "ctx")),
        P(("dp", "ctx")),
        P(("dp", "ctx")),
        P(("dp", "ctx")),
        P("dp", "ctx", None),
    )
    out_specs = (
        P("dp", "ctx", None),
        P("dp", "ctx", None),
        P(("dp", "ctx")),
        P(("dp", "ctx")),
        P(("dp", "ctx")),
        P(("dp", "ctx")),
        P(("dp", "ctx")),
        P(("dp", "ctx")),
        P(("dp", "ctx")),
        P(("dp", "ctx")),
    )
    return jax.shard_map(local, mesh=mesh, in_specs=in_specs, out_specs=out_specs, check_vma=False)
```

profile of v0, /device:TPU:0, one launch (start us, length us, event | category | flops | bytes accessed | tf_op | source)
XLA Modules:
  0.0 1339.3 jit_solution(15277866067685980426)
XLA Ops:
  9.4 64.2 %all-gather.7.cloned.1.call-done = bf16[1769472]{0:T(1024)(128)(2,1)} async-done(((bf16[55296]{0:T(1024)(128)(2,1)}), bf16[1769472]{0:T(1024)(128)(2,1)}) %all-gather.7.cloned.1.call-update) | async-done | bytes 3538960 | tf_op jit(solution)/shard_map/all_gather | solution.py:212
  97.5 39.0 %all-reduce.14 = (bf16[768]{0:T(1024)(128)(2,1)S(1)}, bf16[768]{0:T(1024)(128)(2,1)S(1)}, bf16[768]{0:T(1024)(128)(2,1)S(1)}, bf16[768]{0:T(1024)(128)(2,1)S(1)}) all-reduce(bf16[768]{0:T(1024)(128)(2,1)S(1)} %dynamic-update-slice.1, bf16[768]{0:T(1024)(128)(2,1)S(1)} %dynamic-update-slice, ...), channel_id=1, replica_groups=mesh['dp'=8,'ctx'=4] {'dp','ctx'}, use_global_device_ids=true, to_apply=%add.1 | all-reduce | flops 3072 | bytes 12288
  136.6 9.4 all_gather.43
  150.3 44.6 %all-gather.17.cloned.1.call-done = bf16[2359296]{0:T(1024)(128)(2,1)} async-done(((bf16[73728]{0:T(1024)(128)(2,1)}), bf16[2359296]{0:T(1024)(128)(2,1)}) %all-gather.17.cloned.1.call-update) | async-done | bytes 4718608 | tf_op jit(solution)/shard_map/all_gather | solution.py:215
  194.9 9.3 reshape.270
  204.1 55.0 %all-gather.9.cloned.1.call-done = bf16[2,1024,768]{1,2,0:T(8,128)(2,1)} async-done(((bf16[2,256,768]{1,2,0:T(8,128)(2,1)}), bf16[2,1024,768]{1,2,0:T(8,128)(2,1)}) %all-gather.9.cloned.1.call-update) | async-done | bytes 3145744 | tf_op jit(solution)/shard_map/all_gather | solution.py:242
  259.1 63.6 %all-gather.11.cloned.1.call-done = bf16[2,1024,768]{1,2,0:T(8,128)(2,1)} async-done(((bf16[2,256,768]{1,2,0:T(8,128)(2,1)}), bf16[2,1024,768]{1,2,0:T(8,128)(2,1)}) %all-gather.11.cloned.1.call-update) | async-done | bytes 3145744 | tf_op jit(solution)/shard_map/all_gather | solution.py:241
  322.8 32.1 %while.34 = (s32[]{:T(128)}, bf16[2,256,768]{2,1,0:T(8,128)(2,1)S(1)}, f32[2,12,256]{2,1,0:T(8,128)S(1)}, bf16[2,1024,768]{1,2,0:T(8,128)(2,1)}, bf16[2,256,768]...) while((s32[]{:T(128)}, ...), condition=%wide.region_3.4_spmd.clone, body=%wide.region_0.3_spmd.clone.sunk | while | flops 280558592 | bytes 18917624 | solution.py:141
  358.7 47.0 %all-gather.15.cloned.1.call-done = bf16[4718592]{0:T(1024)(128)(2,1)} async-done(((bf16[147456]{0:T(1024)(128)(2,1)}), bf16[4718592]{0:T(1024)(128)(2,1)}) %all-gather.15.cloned.1.call-update) | async-done | bytes 9437200 | tf_op jit(solution)/shard_map/all_gather | solution.py:214
  405.7 14.0 %reshape.269 = bf16[768,6144]{1,0:T(8,128)(2,1)} reshape(bf16[4718592]{0:T(1024)(128)(2,1)} %all-gather.15.cloned.1.call-done) | data formatting | bytes 18874368 | tf_op jit(solution)/shard_map/reshape | solution.py:91
  419.7 7.8 fusion.53
  438.7 9.0 multiply_convert_fusion.2
  447.7 10.6 multiply_reduce_fusion.1
  466.9 156.2 %while.35 = (s32[]{:T(128)}, f32[2,256,768]{1,2,0:T(8,128)}, bf16[2,1024,768]{1,2,0:T(8,128)(2,1)}, bf16[2,1024,768]{2,1,0:T(8,128)(2,1)}, bf16[2,1024,768]{1,2,...) while((s32[]{:T(128)}, f32[2,256,768]{1,2,0:T(8,128)}, ...), condition=%wide.region_14.15_spmd.clone, body=%wide.region_12.0_spmd.clone.sunk | while | flops 686297088 | bytes 57170232 | solution.py:192
  477.5 7.0 fusion.117
  484.5 6.8 fusion.118
  503.5 7.0 fusion.117
  510.5 6.8 fusion.118
  529.6 7.0 fusion.117
  536.5 6.8 fusion.118
  555.6 7.0 fusion.117
  581.6 7.0 fusion.117
  607.6 7.0 fusion.117
  637.8 10.8 reshape.283
  648.5 8.5 convolution_bitcast_fusion
  657.0 7.5 copy.64
  664.6 17.5 %reduce-scatter.5.cloned.1.call-done = bf16[2,256,768]{2,1,0:T(8,128)(2,1)} async-done(((bf16[2,1024,768]{2,1,0:T(8,128)(2,1)}), bf16[2,256,768]{2,1,0:T(8,128)(2,1)}) %reduce-scatter.5.cloned.1.call-update) | async-done | bytes 786448 | tf_op jit(solution)/shard_map/reduce_scatter | solution.py:315
  683.5 61.2 %reduce-scatter.3.cloned.1.call-done = bf16[2,256,768]{1,2,0:T(8,128)(2,1)} async-done(((bf16[2,1024,768]{1,2,0:T(8,128)(2,1)}), bf16[2,256,768]{1,2,0:T(8,128)(2,1)}) %reduce-scatter.3.cloned.1.call-update) | async-done | bytes 786448 | tf_op jit(solution)/shard_map/reduce_scatter | solution.py:312
  754.6 8.1 copy.41
  762.7 7.9 reshape.280
  771.3 42.6 %all-reduce.12 = (f32[768]{0:T(1024)}, f32[768]{0:T(1024)}, f32[768]{0:T(1024)}, f32[768]{0:T(1024)}) all-reduce(f32[768]{0:T(1024)S(1)} %get-tuple-element.390, f32[768]{0:T(1024)S(1)} %get-tuple-element.395, f32[768]{0:T(1024)S(1)} %get-tuple-element.392, f32[768]{0:T(1024)S(1)} %copy-done.22), channel_id=8, replica_groups=mesh['dp'=8,'ctx'=4] {'dp','ctx'}, use_global_device_ids=true, to_apply=%region_22.23.clone | all-reduce | flops 3072 | bytes 24576
  824.4 501.4 %all-reduce.17.cloned.1.call-done = (f32[1769472]{0:T(1024)}, f32[589824]{0:T(1024)}, f32[4718592]{0:T(1024)}, f32[2359296]{0:T(1024)}) async-done(((f32[1769472]{0:T(1024)}, f32[589824]{0:T(1024)}, f32[4718592]{0:T(1024)}, f32[2359296]{0:T(1024)}), (f32[1769472]{0:T(1024)}, f32[589824]{0:T(1024)}, f32[4718592]{0:T(1024)}, f32[2359296]{0:T(1024)})) %all-reduce.17.cloned.1.call-update) | async-done | bytes 37748752
  (295 shorter events, 222.5 us)
Async XLA Ops:
  7.2 66.5 %all-gather.7.cloned.1.call-start = ((), (), s32[]{:S(2)}) async-start(), calls=%async_computation.2 | async-start | bytes 3649536 | tf_op jit(solution)/shard_map/all_gather | solution.py:212
  7.9 139.0 %all-gather.13.cloned.1.call-start = ((), (), s32[]{:S(2)}) async-start(), calls=%async_computation.5 | async-start | bytes 1216512 | tf_op jit(solution)/shard_map/all_gather | solution.py:213
  8.7 186.2 %all-gather.17.cloned.1.call-start = ((), (), s32[]{:S(2)}) async-start(), calls=%async_computation.7 | async-start | bytes 4866048 | tf_op jit(solution)/shard_map/all_gather | solution.py:215
  9.4 249.7 %all-gather.9.cloned.1.call-start = ((), (), s32[]{:S(2)}) async-start(), calls=%async_computation.3 | async-start | bytes 3932160 | tf_op jit(solution)/shard_map/all_gather | solution.py:242
  80.0 4.0 copy-start.1
  84.0 7.6 copy-start.23
  88.4 2.1 copy-start.11
  91.6 231.2 %all-gather.11.cloned.1.call-start = ((), (), s32[]{:S(2)}) async-start(), calls=%async_computation.4 | async-start | bytes 3932160 | tf_op jit(solution)/shard_map/all_gather | solution.py:241
  92.0 2.3 copy-start.18
  92.0 2.3 copy-start.20
  94.3 2.3 copy-start.26
  94.3 2.5 copy-start.27
  94.3 2.7 copy-start.28
  94.3 2.9 copy-start.29
  94.4 42.2 %copy-start.24 = (s32[2,256]{1,0:T(2,128)S(1)}, s32[2,256]{1,0:T(2,128)}, u32[]{:S(2)}) copy-start(s32[2,256]{1,0:T(2,128)} %param.17) | copy-start | bytes 6148
  94.4 51.6 %copy-start.6 = (bf16[2,256,768]{2,1,0:T(8,128)(2,1)S(1)}, bf16[2,256,768]{2,1,0:T(8,128)(2,1)}, u32[]{:S(2)}) copy-start(bf16[2,256,768]{2,1,0:T(8,128)(2,1)} %param.27) | copy-start | bytes 2359300
  95.9 309.8 %all-gather.15.cloned.1.call-start = ((), (), s32[]{:S(2)}) async-start(), calls=%async_computation.6 | async-start | bytes 9732096 | tf_op jit(solution)/shard_map/all_gather | solution.py:214
  96.5 585.6 %reduce-scatter.5.cloned.1.call-start = ((), (), s32[]{:S(2)}) async-start(), calls=%async_computation.9 | async-start | bytes 3932160 | tf_op jit(solution)/shard_map/reduce_scatter | solution.py:315
  358.4 100.0 %copy-start.3 = (f32[512,768]{1,0:T(8,128)}, f32[512,768]{1,0:T(8,128)S(1)}, u32[]{:S(2)}) copy-start(f32[512,768]{1,0:T(8,128)S(1)} %get-tuple-element.479) | copy-start | bytes 4718596
  430.0 6.2 copy-start.4
  438.7 9.0 copy-start.7
  471.1 2.0 copy-start
  497.2 2.0 copy-start
  623.1 121.6 %reduce-scatter.3.cloned.1.call-start = ((), (), s32[]{:S(2)}) async-start(), calls=%async_computation.8 | async-start | bytes 3932160 | tf_op jit(solution)/shard_map/reduce_scatter | solution.py:312
  623.8 701.9 %all-reduce.17.cloned.1.call-start = ((), (), s32[]{:S(2)}) async-start(), calls=%async_computation.10 | async-start | bytes 75497472
  626.8 4.4 copy-start.5
  664.5 81.5 %copy-start.8 = (f32[2,256,768]{1,2,0:T(8,128)S(1)}, f32[2,256,768]{1,2,0:T(8,128)}, u32[]{:S(2)}) copy-start(f32[2,256,768]{1,2,0:T(8,128)} %get-tuple-element.308) | copy-start | bytes 4718596
  664.6 81.5 %copy-start.19 = (f32[2,256,32]{1,2,0:T(8,128)S(1)}, f32[2,256,32]{1,2,0:T(8,128)}, u32[]{:S(2)}) copy-start(f32[2,256,32]{1,2,0:T(8,128)} %copy-done.18) | copy-start | bytes 196612
  664.6 81.5 %copy-start.21 = (f32[2,256,32]{1,2,0:T(8,128)S(1)}, f32[2,256,32]{1,2,0:T(8,128)}, u32[]{:S(2)}) copy-start(f32[2,256,32]{1,2,0:T(8,128)} %copy-done.20) | copy-start | bytes 196612
  683.5 65.2 %copy-start.15 = (bf16[512,768]{0,1:T(8,128)(2,1)}, bf16[512,768]{0,1:T(8,128)(2,1)S(1)}, u32[]{:S(2)}) copy-start(bf16[512,768]{0,1:T(8,128)(2,1)S(1)} %copy.40) | copy-start | bytes 2359300
  747.5 2.2 copy-start.25
  770.6 48.4 %copy-start.2 = (bf16[768,2304]{1,0:T(8,128)(2,1)S(1)}, bf16[768,2304]{1,0:T(8,128)(2,1)}, u32[]{:S(2)}) copy-start(bf16[768,2304]{1,0:T(8,128)(2,1)} %copy-done.1) | copy-start | bytes 10616836
  (12 other events, 17.3 us)
Sparse Core Ops, SparseCore 0:
  10.8 62.8 all-gather.6
  76.5 53.2 all-gather.12
  132.5 62.2 all-gather.16
  196.9 62.2 all-gather.8
  261.1 61.5 all-gather.10
  325.4 80.2 all-gather.14
  623.2 58.8 reduce-scatter.4
  684.4 60.2 reduce-scatter.2
  770.8 554.9 all-reduce.16
where the time goes:
time: 1350 us; the launch traced here: 1340 us
  waiting for transfers between devices  858 us (64%)
  matrix products  194 us (14%)
  local copies, waits for them, and re-layouts  158 us (12%)
  blocking collectives  91.1 us (7%)
  other arithmetic  22 us (2%)
  between operations  14.6 us (1%)
    unnamed x10, waiting for transfers between devices  505 us
    unnamed x2, blocking collectives  81.7 us
    all_gather x1, waiting for transfers between devices, local(): lax.all_gather(qkv_weight, ('dp', 'ctx'), axis=0, tiled=True)  64.2 us
    all_gather x1, waiting for transfers between devices, local(): lax.all_gather(keys_low, 'ctx', axis=1, tiled=True)  63.6 us
    reduce_scatter x1, waiting for transfers between devices, local(): lax.psum_scatter(key_partial.astype(jnp.bfloat16), 'ctx', scatter_dimensi...  61.2 us
    all_gather x1, waiting for transfers between devices, local(): lax.all_gather(values_low, 'ctx', axis=1, tiled=True)  55 us
    all_gather x1, waiting for transfers between devices, local(): lax.all_gather(gate_up_weight, ('dp', 'ctx'), axis=0, tiled=True)  47 us
    all_gather x1, waiting for transfers between devices, local(): lax.all_gather(down_weight, ('dp', 'ctx'), axis=0, tiled=True)  44.6 us
  transfers between devices with their start and end apart: 9, of which 8 were waited for; matrix products, arithmetic and copies ran while one was open for 9% of the time, Pallas kernels for 0%

commit v1 on v0

--- a/solution.py
+++ b/solution.py
@@ -3,6 +3,8 @@
 import jax
 import jax.numpy as jnp
 from jax import lax
+from jax.experimental import pallas as pl
+from jax.experimental.pallas import tpu as pltpu
 from jax.sharding import PartitionSpec as P
 
 D = 768
@@ -349,6 +351,531 @@
     )
 
 
+PAIR = 2 * HEAD_DIM
+HALF_D = D // 2
+LOG2E = 1.4426950408889634
+BF = jnp.bfloat16
+F32 = jnp.float32
+AXES = ("dp", "ctx")
+
+
+def dot_nn(left, right):
+    return lax.dot_general(left, right, (((1,), (0,)), ((), ())), preferred_element_type=F32)
+
+
+def dot_nt(left, right):
+    return lax.dot_general(left, right, (((1,), (1,)), ((), ())), preferred_element_type=F32)
+
+
+def dot_tn(left, right):
+    return lax.dot_general(left, right, (((0,), (0,)), ((), ())), preferred_element_type=F32)
+
+
+def swap_halves(tile):
+    lane = lax.broadcasted_iota(jnp.int32, tile.shape, 1)
+    low_half = lax.rem(lane, HEAD_DIM) < HEAD_DIM // 2
+    ahead = pltpu.roll(tile, PAIR - HEAD_DIM // 2, 1)
+    behind = pltpu.roll(tile, HEAD_DIM // 2, 1)
+    return jnp.where(low_half, ahead, behind)
+
+
+def qkv_body(x_ref, w_ref, cos_ref, sin_ref, o_ref):
+    product = dot_nn(x_ref[...], w_ref[0])
+    part = pl.program_id(0)
+
+    @pl.when(part < 2)
+    def _():
+        for c in range(HALF_D // PAIR):
+            tile = product[:, c * PAIR : (c + 1) * PAIR]
+            turned = tile * cos_ref[...] + swap_halves(tile) * sin_ref[...]
+            o_ref[:, c * PAIR : (c + 1) * PAIR] = turned.astype(BF)
+
+    @pl.when(part == 2)
+    def _():
+        o_ref[...] = product.astype(BF)
+
+
+def project_qkv(tokens, weight, cosine, sine):
+    rows = tokens.shape[0]
+    tile = 256
+    return pl.pallas_call(
+        qkv_body,
+        out_shape=jax.ShapeDtypeStruct((rows, 3 * HALF_D), BF),
+        grid=(3, rows // tile),
+        in_specs=[
+            pl.BlockSpec((tile, D), lambda i, r: (r, 0)),
+            pl.BlockSpec((1, D, HALF_D), lambda i, r: (i, 0, 0)),
+            pl.BlockSpec((tile, PAIR), lambda i, r: (r, 0)),
+            pl.BlockSpec((tile, PAIR), lambda i, r: (r, 0)),
+        ],
+        out_specs=pl.BlockSpec((tile, HALF_D), lambda i, r: (r, i)),
+        cost_estimate=pl.CostEstimate(
+            flops=2 * rows * D * 3 * HALF_D, bytes_accessed=6 * rows * D, transcendentals=0
+        ),
+        name="project_qkv",
+    )(tokens, weight, cosine, sine)
+
+
+Q_TILE = 256
+
+
+def lane_head(shape):
+    return lax.broadcasted_iota(jnp.int32, shape, 1) // HEAD_DIM
+
+
+def row_head(shape):
+    return lax.broadcasted_iota(jnp.int32, shape, 0) // HEAD_DIM
+
+
+def attend_body(q_ref, k_ref, v_ref, segc_ref, segr_ref, o_ref, l_ref):
+    keys = k_ref[...]
+    values_t = v_ref[...].astype(F32).T.astype(BF)
+    heads_down = row_head(values_t.shape)
+    masked_values = [jnp.where(heads_down == h, values_t, jnp.zeros_like(values_t)) for h in range(2)]
+    rows = q_ref.shape[0]
+    scale = 0.125 * LOG2E
+    for t in range(rows // Q_TILE):
+        span = pl.ds(t * Q_TILE, Q_TILE)
+        queries = q_ref[span, :]
+        heads_across = lane_head(queries.shape)
+        same = segc_ref[...] == segr_ref[:, span]
+        total = jnp.zeros((PAIR, Q_TILE), F32)
+        for h in range(2):
+            scores = dot_nt(keys, jnp.where(heads_across == h, queries, jnp.zeros_like(queries)))
+            scores = jnp.where(same, scores * scale, masked_score)
+            highest = jnp.max(scores, axis=0, keepdims=True)
+            weights = jnp.exp2(scores - highest)
+            norm = jnp.sum(weights, axis=0, keepdims=True)
+            l_ref[0, h : h + 1, span] = highest + jnp.log2(norm)
+            total = total + dot_nn(masked_values[h], weights.astype(BF)) * (1.0 / norm)
+        o_ref[span, :] = total.T.astype(BF)
+
+
+def attend_chip(qkv, seg_col, seg_row):
+    rows = qkv.shape[0]
+    pairs = HALF_D // PAIR
+    return pl.pallas_call(
+        attend_body,
+        out_shape=(
+            jax.ShapeDtypeStruct((rows, HALF_D), BF),
+            jax.ShapeDtypeStruct((pairs, 8, rows), F32),
+        ),
+        grid=(pairs,),
+        in_specs=[
+            pl.BlockSpec((rows, PAIR), lambda p: (0, p)),
+            pl.BlockSpec((rows, PAIR), lambda p: (0, pairs + p)),
+            pl.BlockSpec((rows, PAIR), lambda p: (0, 2 * pairs + p)),
+            pl.BlockSpec((rows, 1), lambda p: (0, 0)),
+            pl.BlockSpec((1, rows), lambda p: (0, 0)),
+        ],
+        out_specs=(
+            pl.BlockSpec((rows, PAIR), lambda p: (0, p)),
+            pl.BlockSpec((1, 8, rows), lambda p: (p, 0, 0)),
+        ),
+        compiler_params=pltpu.CompilerParams(vmem_limit_bytes=48 * 1024 * 1024),
+        cost_estimate=pl.CostEstimate(
+            flops=pairs * 8 * rows * rows * HEAD_DIM,
+            bytes_accessed=8 * rows * HALF_D,
+            transcendentals=2 * pairs * rows * rows,
+        ),
+        name="attend_chip",
+    )(qkv, qkv, qkv, seg_col, seg_row)
+
+
+def attend_back_body(
+    q_ref, k_ref, v_ref, g_ref, l_ref, segc_ref, segr_ref, cos_ref, sin_ref, dq_ref, dk_ref, dv_ref,
+    dk_sum, dv_sum,
+):
+    keys = k_ref[...]
+    values = v_ref[...]
+    keys_t = keys.astype(F32).T.astype(BF)
+    heads_down = row_head(keys_t.shape)
+    masked_keys = [jnp.where(heads_down == h, keys_t, jnp.zeros_like(keys_t)) for h in range(2)]
+    rows = q_ref.shape[0]
+    scale = 0.125 * LOG2E
+    for t in range(rows // Q_TILE):
+        span = pl.ds(t * Q_TILE, Q_TILE)
+        queries = q_ref[span, :]
+        grads = g_ref[span, :]
+        heads_across = lane_head(queries.shape)
+        same = segc_ref[...] == segr_ref[:, span]
+        dq_t = jnp.zeros((PAIR, Q_TILE), F32)
+        dk_part = None
+        dv_part = None
+        for h in range(2):
+            own_q = jnp.where(heads_across == h, queries, jnp.zeros_like(queries))
+            own_g = jnp.where(heads_across == h, grads, jnp.zeros_like(grads))
+            scores = dot_nt(keys, own_q)
+            logits = jnp.where(same, scores * scale, masked_score)
+            probs = jnp.exp2(logits - l_ref[0, h : h + 1, span])
+            prob_grad = dot_nt(values, own_g)
+            mixed = probs * prob_grad
+            mean = jnp.sum(mixed, axis=0, keepdims=True)
+            score_grad = (mixed - probs * mean).astype(BF)
+            dv_new = dot_nn(probs.astype(BF), own_g)
+            dk_new = dot_nn(score_grad, own_q)
+            dv_part = dv_new if dv_part is None else dv_part + dv_new
+            dk_part = dk_new if dk_part is None else dk_part + dk_new
+            dq_t = dq_t + dot_nn(masked_keys[h], score_grad)
+        if t == 0:
+            dk_sum[...] = dk_part
+            dv_sum[...] = dv_part
+        else:
+            dk_sum[...] += dk_part
+            dv_sum[...] += dv_part
+        dq = dq_t.T * 0.125
+        dq_ref[span, :] = (dq * cos_ref[span, :] - swap_halves(dq) * sin_ref[span, :]).astype(BF)
+    dk = dk_sum[...] * 0.125
+    dk_ref[...] = (dk * cos_ref[...] - swap_halves(dk) * sin_ref[...]).astype(BF)
+    dv_ref[...] = dv_sum[...].astype(BF)
+
+
+def attend_back_chip(qkv, grads, totals, seg_col, seg_row, cosine, sine):
+    rows = qkv.shape[0]
+    pairs = HALF_D // PAIR
+    part = jax.ShapeDtypeStruct((rows, HALF_D), BF)
+    column = pl.BlockSpec((rows, PAIR), lambda p: (0, p))
+    whole = pl.BlockSpec((rows, PAIR), lambda p: (0, 0))
+    return pl.pallas_call(
+        attend_back_body,
+        out_shape=(part, part, part),
+        grid=(pairs,),
+        in_specs=[
+            column,
+            pl.BlockSpec((rows, PAIR), lambda p: (0, pairs + p)),
+            pl.BlockSpec((rows, PAIR), lambda p: (0, 2 * pairs + p)),
+            column,
+            pl.BlockSpec((1, 8, rows), lambda p: (p, 0, 0)),
+            pl.BlockSpec((rows, 1), lambda p: (0, 0)),
+            pl.BlockSpec((1, rows), lambda p: (0, 0)),
+            whole,
+            whole,
+        ],
+        out_specs=(column, column, column),
+        scratch_shapes=[pltpu.VMEM((rows, PAIR), F32), pltpu.VMEM((rows, PAIR), F32)],
+        compiler_params=pltpu.CompilerParams(vmem_limit_bytes=56 * 1024 * 1024),
+        cost_estimate=pl.CostEstimate(
+            flops=pairs * 20 * rows * rows * HEAD_DIM,
+            bytes_accessed=16 * rows * HALF_D,
+            transcendentals=2 * pairs * rows * rows,
+        ),
+        name="attend_back_chip",
+    )(qkv, qkv, qkv, grads, totals, seg_col, seg_row, cosine, sine)
+
+
+def at(array, index, axis):
+    return lax.dynamic_index_in_dim(array, index, axis, keepdims=False)
+
+
+class Chip:
+    def __init__(self, side, depth):
+        self.side, self.depth = side, depth
+        place = lax.axis_index("dp")
+        self.k = lax.rem(place, 2)
+        self.x = lax.rem(place // 2, side)
+        self.y = place // (2 * side)
+        self.z = lax.axis_index("ctx")
+
+    def move(self, array, target):
+        pairs = []
+        for y in range(self.side):
+            for x in range(self.side):
+                for k in range(2):
+                    for z in range(self.depth):
+                        ty, tx, tk, tz = target(y, x, k, z)
+                        source = ((y * self.side + x) * 2 + k) * self.depth + z
+                        goal = ((ty * self.side + tx) * 2 + tk) * self.depth + tz % self.depth
+                        pairs.append((source, goal))
+        return lax.ppermute(array, AXES, pairs)
+
+    def core(self, array):
+        return self.move(array, lambda y, x, k, z: (y, x, 1 - k, z))
+
+    def across_x(self, array):
+        return self.move(array, lambda y, x, k, z: (y, 1 - x, k, z))
+
+    def across_y(self, array):
+        return self.move(array, lambda y, x, k, z: (1 - y, x, k, z))
+
+    def up(self, array):
+        return self.move(array, lambda y, x, k, z: (y, x, k, z + 1))
+
+    def down(self, array):
+        return self.move(array, lambda y, x, k, z: (y, x, k, z - 1))
+
+    def order(self, index, own, other, axis=0):
+        own, other = jnp.expand_dims(own, axis), jnp.expand_dims(other, axis)
+        shape = [1] * own.ndim
+        shape[axis] = 2
+        return jnp.where(jnp.arange(2).reshape(shape) == index, own, other)
+
+    def gather_x(self, array, axis=0):
+        return self.order(self.x, array, self.across_x(array), axis)
+
+    def gather_y(self, array, axis=0):
+        return self.order(self.y, array, self.across_y(array), axis)
+
+    def ring_z(self, array):
+        half = array.shape[0] // 2
+        below, above = self.up(array), self.down(array)
+        far_a = self.up(below[:half])
+        far_b = self.down(above[half:])
+        return (array, above, jnp.concatenate([far_a, far_b], 0), below)
+
+    def gather_z(self, array, axis=0):
+        pieces = self.ring_z(array)
+        shape = list(array.shape)
+        shape.insert(axis, self.depth)
+        result = jnp.zeros(shape, array.dtype)
+        for step, piece in enumerate(pieces):
+            place = lax.rem(self.z + step, self.depth)
+            result = lax.dynamic_update_index_in_dim(result, piece, place, axis)
+        return result
+
+    def scatter(self, array, index, across, axis):
+        own = at(array, index, axis)
+        got = across(at(array, 1 - index, axis).astype(BF))
+        return own.astype(F32) + got.astype(F32)
+
+    def scatter_x(self, array, axis=0):
+        return self.scatter(array, self.x, self.across_x, axis)
+
+    def scatter_y(self, array, axis=0):
+        return self.scatter(array, self.y, self.across_y, axis)
+
+    def scatter_z(self, array, axis=0):
+        def share(step):
+            return at(array, lax.rem(self.z + step, self.depth), axis)
+
+        far = share(2).astype(BF)
+        half = far.shape[0] // 2
+        first = self.up(far[:half])
+        second = self.down(far[half:])
+        above, below = share(1), share(3)
+        sum_above = (above[:half].astype(F32) + first.astype(F32)).astype(BF)
+        sum_below = (below[half:].astype(F32) + second.astype(F32)).astype(BF)
+        got_a = self.up(jnp.concatenate([sum_above, above[half:].astype(BF)], 0))
+        got_b = self.down(jnp.concatenate([below[:half].astype(BF), sum_below], 0))
+        return share(0).astype(F32) + got_a.astype(F32) + got_b.astype(F32)
+
+
+def to_sequence(chip, blocks):
+    got = []
+    for r in range(2):
+        j = lax.rem(chip.z + r, 2)
+        got.append(
+            chip.move(at(blocks, j, 0), lambda y, x, k, z, r=r: (y, x, z // 2, 2 * k + (r + z) % 2))
+        )
+    odd = lax.rem(chip.z, 2)
+    return chip.order(odd, got[0], got[1])
+
+
+def from_sequence(chip, halves):
+    got = []
+    for r in range(2):
+        s = lax.rem(chip.z + r, 2)
+        got.append(
+            chip.move(at(halves, s, 0), lambda y, x, k, z, r=r: (y, x, z // 2, 2 * k + (z + r) % 2))
+        )
+    odd = lax.rem(chip.z, 2)
+    return chip.order(odd, got[0], got[1])
+
+
+def chip_local(
+    tokens,
+    segments,
+    positions,
+    qkv_weight,
+    out_weight,
+    gate_up_weight,
+    down_weight,
+    first_gain,
+    first_bias,
+    second_gain,
+    second_bias,
+    output_grad,
+):
+    depth = lax.axis_size("ctx")
+    side = math.isqrt(lax.axis_size("dp") // 2)
+    chip = Chip(side, depth)
+    k, z = chip.k, chip.z
+    quarter = tokens.shape[1]
+    rows = depth * quarter
+    half = rows // 2
+    owners = 2 * side * side * depth
+    d_rows, ff_rows = D // owners, FF // owners
+    planes = side * side
+    ff_cols = FF // (2 * planes)
+    ff_half = FF // 2
+
+    extra = jnp.stack(
+        [segments, positions // 32, lax.rem(positions, 32)], axis=1
+    ).astype(BF)
+    extra = jnp.pad(extra, ((0, 0), (0, 13), (0, D - quarter)))
+    own_tokens = to_sequence(chip, jnp.concatenate([tokens, extra], axis=1))
+
+    qkv_own = qkv_weight.reshape(d_rows, 3, 2, HALF_D)
+    gate_up_own = gate_up_weight.reshape(d_rows, 2, planes, 2, ff_cols)
+
+    def column_half(core):
+        q = at(qkv_own, core, 2).reshape(d_rows, 3 * HALF_D)
+        g = at(gate_up_own, core, 3).reshape(d_rows, FF)
+        return jnp.concatenate([q, g], axis=1)
+
+    shard = chip.order(k, column_half(k), chip.core(column_half(1 - k)))
+    qkv_block = shard[:, :, : 3 * HALF_D].reshape(2, d_rows, 3, HALF_D).transpose(2, 0, 1, 3)
+    gate_up_block = shard[:, :, 3 * HALF_D :]
+
+    qkv_z = chip.gather_z(qkv_block.reshape(6 * d_rows, HALF_D)).reshape(depth, 3, 2, d_rows, HALF_D)
+    qkv_a = chip.gather_y(chip.gather_x(qkv_z[:, :, 0]), 0)
+    qkv_b = chip.gather_x(chip.gather_y(qkv_z[:, :, 1]), 1)
+    qkv_mat = jnp.stack([qkv_a, qkv_b], axis=2).transpose(4, 0, 1, 2, 3, 5, 6)
+    qkv_mat = qkv_mat.reshape(3, D, HALF_D)
+
+    both = chip.order(k, own_tokens, chip.core(own_tokens)).reshape(depth, quarter + 16, D)
+    all_tokens = both[:, :quarter].reshape(rows, D)
+    all_extra = both[:, quarter:, :quarter].astype(F32)
+    seg_all = all_extra[:, 0].reshape(rows)
+    pos_all = (all_extra[:, 1] * 32.0 + all_extra[:, 2]).reshape(rows)
+    token_half = own_tokens[:, :quarter].reshape(half, D)
+    lane = jnp.arange(PAIR)
+    counter = lax.rem(lane, HEAD_DIM // 2).astype(F32)
+    inverse = jnp.exp(counter * (-2.0 * math.log(rotary_base) / HEAD_DIM))
+    angles = pos_all[:, None] * inverse
+    cosine = jnp.cos(angles)
+    sine = jnp.where(lax.rem(lane, HEAD_DIM) < HEAD_DIM // 2, -1.0, 1.0) * jnp.sin(angles)
+    seg_col, seg_row = seg_all[:, None], seg_all[None, :]
+
+    gate_up_xy = chip.gather_y(chip.gather_x(gate_up_block))
+    gate_up_xy = gate_up_xy.reshape(planes * 2, d_rows, FF)
+    gate_up_mat = chip.gather_z(gate_up_xy, 1).reshape(D, FF)
+
+    norms = jnp.concatenate([first_gain, first_bias, second_gain, second_bias])
+    norm_rows = jnp.pad(norms[None], ((0, 7), (0, D - 4 * d_rows)))
+    shared = jnp.concatenate(
+        [down_weight.reshape(ff_rows, D), out_weight.reshape(d_rows, D), norm_rows], axis=0
+    )
+    mid = shared.shape[0] // 2
+    shared_z = chip.gather_z(shared)
+    shared_a = chip.gather_y(chip.gather_x(shared_z[:, :mid]))
+    shared_b = chip.gather_x(chip.gather_y(shared_z[:, mid:]), 1)
+    shared_all = jnp.concatenate([shared_a, shared_b], axis=3)
+    down_mat = shared_all[:, :, :, :ff_rows].reshape(ff_half, D)
+    rest = shared_all[:, :, :, ff_rows:]
+    rest = chip.order(k, rest, chip.core(rest), 2)
+    out_mat = rest[..., :d_rows, :].reshape(D, D)
+    norms_all = rest[..., d_rows, : 4 * d_rows].reshape(owners, 4, d_rows)
+    norms_all = norms_all.transpose(1, 0, 2).reshape(4, D).astype(F32)
+    gain_one, bias_one, gain_two, bias_two = (norms_all[i] for i in range(4))
+
+    grad_half = to_sequence(chip, output_grad).reshape(half, D).astype(F32)
+
+    qkv = project_qkv(all_tokens, qkv_mat, cosine, sine)
+    attended, totals = attend_chip(qkv, seg_col, seg_row)
+    parts = attended.reshape(2, half, HALF_D)
+    other = chip.core(at(parts, 1 - k, 0))
+    attended_rows = chip.order(k, at(parts, k, 0), other, 1).reshape(half, D)
+    branch = dot_nn(attended_rows, out_mat)
+    normed_one, hat_one, recip_one = layer_norm(token_half.astype(F32) + branch, gain_one, bias_one)
+    normed_own = normed_one.astype(BF)
+    normed_low = chip.order(k, normed_own, chip.core(normed_own)).reshape(rows, D)
+    gate_up = dot_nn(normed_low, gate_up_mat)
+    gate_part, up_part = gate_up[:, :ff_half], gate_up[:, ff_half:]
+    sigmoid_gate = jax.nn.sigmoid(gate_part)
+    silu_gate = gate_part * sigmoid_gate
+    hidden = (silu_gate * up_part).astype(BF)
+
+    def sum_cores(left, right):
+        both_parts = left.reshape(2, half, left.shape[1])
+        product = right(at(both_parts, 1 - k, 0)).astype(BF)
+        got = chip.core(product)
+        return right(at(both_parts, k, 0)) + got.astype(F32)
+
+    mlp_out = sum_cores(hidden, lambda part: dot_nn(part, down_mat))
+    result, hat_two, recip_two = layer_norm(normed_one + mlp_out, gain_two, bias_two)
+    output = from_sequence(chip, result.astype(BF).reshape(2, quarter, D))
+
+    second_grad, second_gain_part, second_bias_part = norm_back(
+        grad_half, hat_two, recip_two, gain_two
+    )
+    mlp_own = second_grad.astype(BF)
+    mlp_grad = chip.order(k, mlp_own, chip.core(mlp_own)).reshape(rows, D)
+    hidden_grad = dot_nt(mlp_grad, down_mat)
+    gate_grad = hidden_grad * up_part * (sigmoid_gate * (1.0 + gate_part * (1.0 - sigmoid_gate)))
+    up_grad = hidden_grad * silu_gate
+    gate_up_grad = jnp.concatenate([gate_grad, up_grad], axis=1).astype(BF)
+    gate_up_part = dot_tn(normed_low, gate_up_grad).astype(BF)
+    down_part = dot_tn(hidden, mlp_grad).astype(BF)
+
+    gate_up_z = chip.scatter_z(gate_up_part.reshape(planes * 2, depth, d_rows, FF), 1)
+    gate_up_y = chip.scatter_y(gate_up_z.reshape(side, side, 2, d_rows, FF))
+    gate_up_x = chip.scatter_x(gate_up_y)
+    gate_up_got = chip.core(at(gate_up_x, 1 - k, 0).astype(BF)).astype(F32)
+    gate_up_share = chip.order(
+        k,
+        at(gate_up_x, k, 0).reshape(d_rows, 2, planes, ff_cols),
+        gate_up_got.reshape(d_rows, 2, planes, ff_cols),
+        3,
+    ).reshape(-1)
+
+    normed_grad = second_grad + sum_cores(gate_up_grad, lambda part: dot_nt(part, gate_up_mat))
+    first_grad, first_gain_part, first_bias_part = norm_back(
+        normed_grad, hat_one, recip_one, gain_one
+    )
+    branch_grad = first_grad.astype(BF)
+    out_part = dot_tn(attended_rows, branch_grad)
+    attended_own = dot_nt(branch_grad, out_mat).astype(BF).reshape(half, 2, HALF_D)
+    attended_got = chip.core(at(attended_own, 1 - k, 1))
+    attended_grad = chip.order(k, at(attended_own, k, 1), attended_got).reshape(rows, HALF_D)
+
+    norm_parts = jnp.stack([first_gain_part, first_bias_part, second_gain_part, second_bias_part])
+    norm_parts = norm_parts.reshape(4, owners, d_rows).transpose(1, 0, 2).reshape(owners, 1, 4 * d_rows)
+    norm_parts = jnp.pad(norm_parts, ((0, 0), (0, 7), (0, D - 4 * d_rows)))
+    rest_part = jnp.concatenate([out_part.reshape(owners, d_rows, D), norm_parts], axis=1)
+    rest_part = rest_part.reshape(side, side, 2, depth, d_rows + 8, D).astype(BF)
+    rest_own = at(rest_part, k, 2).astype(F32) + chip.core(at(rest_part, 1 - k, 2)).astype(F32)
+    shared_part = jnp.concatenate(
+        [down_part.reshape(side, side, depth, ff_rows, D), rest_own.astype(BF)], axis=3
+    )
+    part_a = chip.scatter_y(chip.scatter_x(shared_part[:, :, :, :mid], 1).astype(BF))
+    part_b = chip.scatter_x(chip.scatter_y(shared_part[:, :, :, mid:], 0).astype(BF))
+    shared_share = chip.scatter_z(jnp.concatenate([part_a, part_b], axis=1).astype(BF))
+    down_share = shared_share[:ff_rows].reshape(-1)
+    out_share = shared_share[ff_rows : ff_rows + d_rows].reshape(-1)
+    norm_share = shared_share[ff_rows + d_rows, : 4 * d_rows].reshape(4, d_rows)
+
+    dq, dk, dv = attend_back_chip(qkv, attended_grad, totals, seg_col, seg_row, cosine, sine)
+    projected_grad = jnp.concatenate([dq, dk, dv], axis=1)
+    qkv_part = dot_tn(all_tokens, projected_grad).astype(BF)
+    qkv_part = qkv_part.reshape(side, side, 2, depth, d_rows, 3 * HALF_D)
+    qkv_pa = chip.scatter_y(chip.scatter_x(qkv_part[:, :, 0], 1).astype(BF))
+    qkv_pb = chip.scatter_x(chip.scatter_y(qkv_part[:, :, 1], 0).astype(BF))
+    qkv_sum = chip.scatter_z(jnp.stack([qkv_pa, qkv_pb], axis=1).astype(BF))
+    qkv_got = chip.core(at(qkv_sum, 1 - k, 0).astype(BF)).astype(F32)
+    qkv_share = chip.order(
+        k,
+        at(qkv_sum, k, 0).reshape(d_rows, 3, HALF_D),
+        qkv_got.reshape(d_rows, 3, HALF_D),
+        2,
+    ).reshape(-1)
+
+    flat_weight = qkv_mat.transpose(1, 0, 2).reshape(D, 3 * HALF_D)
+    input_half = first_grad + sum_cores(projected_grad, lambda part: dot_nt(part, flat_weight))
+    input_grad = from_sequence(chip, input_half.astype(BF).reshape(2, quarter, D)).astype(F32)
+    return (
+        output,
+        input_grad,
+        qkv_share,
+        out_share,
+        gate_up_share,
+        down_share,
+        norm_share[0],
+        norm_share[1],
+        norm_share[2],
+        norm_share[3],
+    )
+
+
 def solution(mesh):
     in_specs = (
         P("dp", "ctx", None),
@@ -376,4 +903,7 @@
         P(("dp", "ctx")),
         P(("dp", "ctx")),
     )
-    return jax.shard_map(local, mesh=mesh, in_specs=in_specs, out_specs=out_specs, check_vma=False)
+    planes = mesh.shape["dp"] // 2
+    fits = planes == 4 and mesh.shape["ctx"] == 4
+    body = chip_local if fits else local
+    return jax.shard_map(body, mesh=mesh, in_specs=in_specs, out_specs=out_specs, check_vma=False)

time: 1350 us -> 529 us (0.39)
  waiting for transfers between devices: 858 us -> 176 us
  matrix products: 194 us -> 47.3 us
  starting transfers between devices: 0.35 us -> 98.4 us
  blocking collectives: 91.1 us -> 0 us
  local copies, waits for them, and re-layouts: 158 us -> 81.9 us
  Pallas kernels: 0 us -> 53.4 us
  other arithmetic: 22 us -> 62.2 us
    unnamed x10 -> x0, waiting for transfers between devices: 505 us -> none
    all_gather x6 -> x0, waiting for transfers between devices: 274 us -> none  [the longest x1 64.2 us: local(): lax.all_gather(qkv_weight, ('dp', 'ctx'), axis=0, tiled=True)]
    ppermute x0 -> x65, waiting for transfers between devices: none -> 176 us  [move(): return lax.ppermute(array, AXES, pairs)]
    dot_general x54 -> x14, matrix products: 194 us -> 47.3 us  [the longest x6 18.8 us: dot_nt(): lax.dot_general(left, right, (((1,), (1,)), ((), ())), preferred_element_...]
    ppermute x0 -> x65, starting transfers between devices: none -> 98.4 us  [move(): return lax.ppermute(array, AXES, pairs)]
    unnamed x2 -> x0, blocking collectives: 81.7 us -> none
    reduce_scatter x2 -> x0, waiting for transfers between devices: 78.7 us -> none  [the longest x1 61.2 us: local(): lax.psum_scatter(key_partial.astype(jnp.bfloat16), 'ctx', scatter_dimensi...]
    pallas_call x0 -> x3, Pallas kernels: none -> 53.4 us  [the longest x1 22.6 us: attend_back_chip(): pl.pallas_call(attend_back_body, out_shape=(part, part, part), grid=(pair...]
  transfers between devices with their start and end apart: 9 -> 65, of which waited for: 8 -> 31; matrix products, arithmetic and copies ran while one was open for 9% -> 31% of each run, Pallas kernels for 0% -> 10%
where the time goes in v1:
time: 529 us; the launch traced here: 522 us
  waiting for transfers between devices  176 us (33%)
  starting transfers between devices  98.4 us (19%)
  local copies, waits for them, and re-layouts  81.9 us (15%)
  other arithmetic  62.2 us (12%)
  Pallas kernels  53.4 us (10%)
  matrix products  47.3 us (9%)
    ppermute x65, waiting for transfers between devices, move(): return lax.ppermute(array, AXES, pairs)  176 us
    ppermute x65, starting transfers between devices, move(): return lax.ppermute(array, AXES, pairs)  98.4 us
    select_n x22, other arithmetic, order(): return jnp.where(jnp.arange(2).reshape(shape) == index, own, other)  23.3 us
    pallas_call x1, Pallas kernels, attend_back_chip(): pl.pallas_call(attend_back_body, out_shape=(part, part, part), grid=(pair...  22.6 us
    unnamed x137, local copies, waits for them, and re-layouts  19.1 us
    dot_general x6, matrix products, dot_nt(): lax.dot_general(left, right, (((1,), (1,)), ((), ())), preferred_element_...  18.8 us
    pallas_call x1, Pallas kernels, attend_chip(): pl.pallas_call(attend_body, out_shape=(jax.ShapeDtypeStruct((rows, HALF_D...  18.5 us
    broadcast_in_dim x23, local copies, waits for them, and re-layouts, order(): return jnp.where(jnp.arange(2).reshape(shape) == index, own, other)  17.9 us
  transfers between devices with their start and end apart: 65, of which 31 were waited for; matrix products, arithmetic and copies ran while one was open for 31% of the time, Pallas kernels for 10%

profile of v1, /device:TPU:0, one launch (start us, length us, event | category | flops | bytes accessed | tf_op | source)
XLA Modules:
  0.0 521.8 jit_solution(7277371625312929811)
XLA Ops:
  3.4 5.1 collective-permute-start.13
  10.6 4.5 collective-permute-start.32
  26.5 15.9 %collective-permute-done.16 = bf16[64,768]{1,0:T(8,128)(2,1)S(1)} collective-permute-done((bf16[64,768]{1,0:T(8,128)(2,1)S(1)}, bf16[64,768]{1,0:T(8,128)(2,1)S(1)}, u32[]{:S(2)}, u32[]{:S(2)}) %collective-permute-start.16) | collective-permute-done | bytes 98336 | tf_op jit(solution)/shard_map/ppermute | solution.py:589
  43.8 5.2 collective-permute-start.5
  75.2 4.2 collective-permute-done.10
  85.4 5.6 %collective-permute-start.2 = (bf16[2,272,768]{2,1,0:T(8,128)(2,1)S(1)}, bf16[2,272,768]{2,1,0:T(8,128)(2,1)S(1)}, u32[]{:S(2)}, u32[]{:S(2)}) collective-permute-start(bf16[2,272,768]{2,1,0:T(8,128)(2,1)S(1)} %broadcast_select_fusion.8), channel_id=1, source_target_pairs={{0,4},{1,5},{2,6},{3,7},{4,0},{5,1},{6,2},{7,3},{8,12},{9,13},{10,... | collective-permute-start | bytes 2506760 | tf_op jit(solution)/shard_map/ppermute | solution.py:589
  97.3 5.9 %collective-permute-done.11 = bf16[2,4,3,24,384]{4,3,1,0,2:T(8,128)(2,1)S(1)} collective-permute-done((bf16[2,4,3,24,384]{4,3,1,0,2:T(8,128)(2,1)S(1)}, bf16[2,4,3,24,384]{4,3,1,0,2:T(8,128)(2,1)S(1)}, u32[]{:S(2)}, u32[]{:S(2)}) %collective-permute-start.11) | collective-permute-done | bytes 442400 | tf_op jit(solution)/shard_map/ppermute | solution.py:589
  109.8 8.7 %collective-permute-done.22 = bf16[2,2,24,3072]{3,2,1,0:T(8,128)(2,1)S(1)} collective-permute-done((bf16[2,2,24,3072]{3,2,1,0:T(8,128)(2,1)S(1)}, bf16[2,2,24,3072]{3,2,1,0:T(8,128)(2,1)S(1)}, u32[]{:S(2)}, u32[]{:S(2)}) %collective-permute-start.22) | collective-permute-done | bytes 589856 | tf_op jit(solution)/shard_map/ppermute | solution.py:589
  124.5 6.1 %collective-permute-start.23 = (bf16[8,24,3072]{2,1,0:T(8,128)(2,1)}, bf16[8,24,3072]{2,1,0:T(8,128)(2,1)}, u32[]{:S(2)}, u32[]{:S(2)}) collective-permute-start(bf16[8,24,3072]{2,1,0:T(8,128)(2,1)} %bitcast_select_fusion.2), channel_id=1, source_target_pairs={{0,3},{1,0},{2,1},{3,2},{4,7},{5,4},{6,5},{7,6},{8,11},{9,8},{10,9... | collective-permute-start | bytes 3538952 | tf_op jit(solution)/shard_map/ppermute | solution.py:589
  133.4 4.4 broadcast_in_dim.701
  143.9 12.4 %project_qkv.1.q_ref.k_ref.v_ref = bf16[1024,1152]{1,0:T(8,128)(2,1)} custom-call(bf16[1024,768]{1,0:T(8,128)(2,1)} %bitcast.402, bf16[3,768,384]{2,1,0:T(8,128)(2,1)} %bitcast.396, f32[1024,128]{1,0:T(8,128)} %get-tuple-element.81.cos_ref, f32[1024,128]{1,0:T(8,128)} %get-tuple-element.80.sin_ref), custom_call_target="tpu_custom_call" | custom-call | flops 1811939328 | bytes 4718592 | tf_op jit(solution)/shard_map/project_qkv/pallas_call | solution.py:401
  158.0 18.5 %attend_chip.1 = (bf16[1024,384]{1,0:T(8,128)(2,1)S(1)}, f32[3,8,1024]{2,1,0:T(8,128)S(1)}) custom-call(bf16[1024,1152]{1,0:T(8,128)(2,1)S(1)} %copy-done, bf16[1024,1152]{1,0:T(8,128)(2,1)S(1)} %copy-done, bf16[1024,1152]{1,0:T(8,128)(2,1)S(1)} %copy-done, f32[1024,1]{1,0:T(8,128)S(1)} %bitcast.388, f32[1,1024]{1,0:T(1,128)S(1)} %bitcast.391), custom_call_target="tpu_custom_call" | custom-call | flops 1610612736 | bytes 3145728 | tf_op jit(solution)/shard_map/attend_chip/pallas_call | solution.py:457
  196.2 17.6 %collective-permute-done.24 = bf16[8,24,3072]{2,1,0:T(8,128)(2,1)} collective-permute-done((bf16[8,24,3072]{2,1,0:T(8,128)(2,1)}, bf16[8,24,3072]{2,1,0:T(8,128)(2,1)}, u32[]{:S(2)}, u32[]{:S(2)}) %collective-permute-start.24) | collective-permute-done | bytes 1179680 | tf_op jit(solution)/shard_map/ppermute | solution.py:589
  217.4 9.0 %collective-permute-done.26 = bf16[4,24,3072]{2,1,0:T(8,128)(2,1)S(1)} collective-permute-done((bf16[4,24,3072]{2,1,0:T(8,128)(2,1)S(1)}, bf16[4,24,3072]{2,1,0:T(8,128)(2,1)S(1)}, u32[]{:S(2)}, u32[]{:S(2)}) %collective-permute-start.26) | collective-permute-done | bytes 589856 | tf_op jit(solution)/shard_map/ppermute | solution.py:589
  226.4 11.7 %collective-permute-done.25 = bf16[4,24,3072]{2,1,0:T(8,128)(2,1)S(1)} collective-permute-done((bf16[4,24,3072]{2,1,0:T(8,128)(2,1)S(1)}, bf16[4,24,3072]{2,1,0:T(8,128)(2,1)S(1)}, u32[]{:S(2)}, u32[]{:S(2)}) %collective-permute-start.25) | collective-permute-done | bytes 589856 | tf_op jit(solution)/shard_map/ppermute | solution.py:589
  242.5 6.9 %fusion.118 = f32[1024,3072]{1,0:T(8,128)S(1)} fusion(bf16[1024,768]{1,0:T(8,128)(2,1)S(1)} %bitcast.427, bf16[768,3072]{1,0:T(8,128)(2,1)} %bitcast.408), kind=kOutput, calls=%fused_computation.318 | convolution fusion | flops 4831838208 | bytes 18874368 | tf_op jit(solution)/shard_map/dot_general | solution.py:363
  274.6 4.6 collective-permute-start.30
  281.3 7.4 %multiply_convert_fusion = (bf16[1024,1536]{1,0:T(8,128)(2,1)S(1)}, bf16[1024,1536]{1,0:T(8,128)(2,1)S(1)}) fusion(f32[1024,3072]{1,0:T(8,128)} %copy-done.7, bf16[1024,768]{1,0:T(8,128)(2,1)S(1)} %bitcast.426, bf16[1536,768]{1,0:T(8,128)(2,1)S(1)} %bitcast.421), kind=kOutput, calls=%fused_computation.8 | convolution fusion | flops 2436366336 | bytes 22806528 | tf_op jit(solution)/shard_map/dot_general | solution.py:367
  300.5 7.3 %fusion.5 = bf16[768,3072]{1,0:T(8,128)(2,1)S(1)} fusion(bf16[1024,768]{1,0:T(8,128)(2,1)S(1)} %get-tuple-element.84, bf16[1024,1536]{1,0:T(8,128)(2,1)S(1)} %copy-done.58, bf16[1024,1536]{1,0:T(8,128)(2,1)} %copy-done.60), kind=kOutput, calls=%fused_computation.13 | convolution fusion | flops 4846780416 | bytes 12582912 | tf_op jit(solution)/shard_map/dot_general | solution.py:371
  313.0 13.3 %collective-permute-done.58 = bf16[4,24,3072]{2,1,0:T(8,128)(2,1)S(1)} collective-permute-done((bf16[4,24,3072]{2,1,0:T(8,128)(2,1)S(1)}, bf16[4,24,3072]{2,1,0:T(8,128)(2,1)S(1)}, u32[]{:S(2)}, u32[]{:S(2)}) %collective-permute-start.58) | collective-permute-done | bytes 589856 | tf_op jit(solution)/shard_map/ppermute | solution.py:589
  327.7 10.3 %collective-permute-done.60 = bf16[4,24,3072]{2,1,0:T(8,128)(2,1)S(1)} collective-permute-done((bf16[4,24,3072]{2,1,0:T(8,128)(2,1)S(1)}, bf16[4,24,3072]{2,1,0:T(8,128)(2,1)S(1)}, u32[]{:S(2)}, u32[]{:S(2)}) %collective-permute-start.60) | collective-permute-done | bytes 589856 | tf_op jit(solution)/shard_map/ppermute | solution.py:589
  343.0 4.6 multiply_reduce_fusion
  362.2 22.6 %attend_back_chip.1 = (bf16[1024,384]{1,0:T(8,128)(2,1)}, bf16[1024,384]{1,0:T(8,128)(2,1)}, bf16[1024,384]{1,0:T(8,128)(2,1)}) custom-call(bf16[1024,1152]{1,0:T(8,128)(2,1)} %project_qkv.1.q_ref.k_ref.v_ref, bf16[1024,1152]{1,0:T(8,128)(2,1)} %project_qkv.1.q_ref.k_ref.v_ref, bf16[1024,1152]{1,0:T(8,128)(2,1)} %project_qkv.1.q_ref.k_ref.v_ref, ...), custom_call_target="tpu_custom_call" | custom-call | flops 4026531840 | bytes 6291456 | tf_op jit(solution)/shard_map/attend_back_chip/pallas_call | solution.py:539
  394.8 7.6 %collective-permute-done.40 = bf16[2,4,24,1152]{3,2,1,0:T(8,128)(2,1)S(1)} collective-permute-done((bf16[2,4,24,1152]{3,2,1,0:T(8,128)(2,1)S(1)}, bf16[2,4,24,1152]{3,2,1,0:T(8,128)(2,1)S(1)}, u32[]{:S(2)}, u32[]{:S(2)}) %collective-permute-start.40) | collective-permute-done | bytes 442400 | tf_op jit(solution)/shard_map/ppermute | solution.py:589
  404.1 9.6 %collective-permute-done.42 = bf16[2,4,24,1152]{3,2,1,0:T(8,128)(2,1)S(1)} collective-permute-done((bf16[2,4,24,1152]{3,2,1,0:T(8,128)(2,1)S(1)}, bf16[2,4,24,1152]{3,2,1,0:T(8,128)(2,1)S(1)}, u32[]{:S(2)}, u32[]{:S(2)}) %collective-permute-start.42) | collective-permute-done | bytes 442400 | tf_op jit(solution)/shard_map/ppermute | solution.py:589
  435.9 4.5 collective-permute-start.38
  457.2 6.8 %collective-permute-start.51 = (bf16[2,2,4,32,768]{4,3,2,1,0:T(8,128)(2,1)S(1)}, bf16[2,2,4,32,768]{4,3,2,1,0:T(8,128)(2,1)S(1)}, u32[]{:S(2)}, u32[]{:S(2)}) collective-permute-start(bf16[2,2,4,32,768]{4,3,2,1,0:T(8,128)(2,1)S(1)} %dynamic-slice_bitcast_fusion.1), channel_id=1, source_target_pairs={{0,4},{1,5},{2,6},{3,7},{4,0},{5,1},{6,2},{7,3},{8,12},{9,13},{10,... | collective-permute-start | bytes 2359304 | tf_op jit(solution)/shard_map/ppermute | solution.py:589
  470.5 5.5 %collective-permute-done.63 = bf16[2,24,3072]{2,1,0:T(8,128)(2,1)} collective-permute-done((bf16[2,24,3072]{2,1,0:T(8,128)(2,1)}, bf16[2,24,3072]{2,1,0:T(8,128)(2,1)}, u32[]{:S(2)}, u32[]{:S(2)}) %collective-permute-start.63) | collective-permute-done | bytes 294944 | tf_op jit(solution)/shard_map/ppermute | solution.py:589
  477.2 12.2 %collective-permute-done.52 = bf16[2,4,64,768]{3,2,1,0:T(8,128)(2,1)} collective-permute-done((bf16[2,4,64,768]{3,2,1,0:T(8,128)(2,1)}, bf16[2,4,64,768]{3,2,1,0:T(8,128)(2,1)}, u32[]{:S(2)}, u32[]{:S(2)}) %collective-permute-start.52) | collective-permute-done | bytes 786464 | tf_op jit(solution)/shard_map/ppermute | solution.py:589
  493.9 9.0 %collective-permute-done.53 = bf16[4,64,768]{2,1,0:T(8,128)(2,1)S(1)} collective-permute-done((bf16[4,64,768]{2,1,0:T(8,128)(2,1)S(1)}, bf16[4,64,768]{2,1,0:T(8,128)(2,1)S(1)}, u32[]{:S(2)}, u32[]{:S(2)}) %collective-permute-start.53) | collective-permute-done | bytes 393248 | tf_op jit(solution)/shard_map/ppermute | solution.py:589
  505.2 4.5 collective-permute-done.56
  513.6 5.6 %collective-permute-done.57 = bf16[128,768]{1,0:T(8,128)(2,1)S(1)} collective-permute-done((bf16[128,768]{1,0:T(8,128)(2,1)S(1)}, bf16[128,768]{1,0:T(8,128)(2,1)S(1)}, u32[]{:S(2)}, u32[]{:S(2)}) %collective-permute-start.57) | collective-permute-done | bytes 196640 | tf_op jit(solution)/shard_map/ppermute | solution.py:589
  (457 shorter events, 241.8 us)
Async XLA Ops:
  3.4 18.2 %collective-permute-start.13 = (bf16[128,768]{1,0:T(8,128)(2,1)S(1)}, bf16[128,768]{1,0:T(8,128)(2,1)S(1)}, u32[]{:S(2)}, u32[]{:S(2)}) collective-permute-start(bf16[128,768]{1,0:T(8,128)(2,1)S(1)} %fusion.78), channel_id=1, source_target_pairs={{0,3},{1,0},{2,1},{3,2},{4,7},{5,4},{6,5},{7,6},{8,11},{9,8},{10,9... | collective-permute-start | bytes 589832 | tf_op jit(solution)/shard_map/ppermute | solution.py:589
  10.6 246.3 %collective-permute-start.33 = (bf16[256,768]{1,0:T(8,128)(2,1)}, bf16[256,768]{1,0:T(8,128)(2,1)}, u32[]{:S(2)}, u32[]{:S(2)}) collective-permute-start(bf16[256,768]{1,0:T(8,128)(2,1)} %get-tuple-element.58), channel_id=1, source_target_pairs={{0,1},{1,0},{2,5},{3,4},{4,3},{5,2},{6,7},{7,6},{8,9},{9,8},{10,13... | collective-permute-start | bytes 1179656 | tf_op jit(solution)/shard_map/ppermute | solution.py:589
  10.6 246.3 %collective-permute-start.32 = (bf16[256,768]{1,0:T(8,128)(2,1)}, bf16[256,768]{1,0:T(8,128)(2,1)}, u32[]{:S(2)}, u32[]{:S(2)}) collective-permute-start(bf16[256,768]{1,0:T(8,128)(2,1)} %get-tuple-element.57), channel_id=1, source_target_pairs={{0,0},{1,1},{2,4},{3,5},{4,2},{5,3},{6,6},{7,7},{8,8},{9,9},{10,12... | collective-permute-start | bytes 1179656 | tf_op jit(solution)/shard_map/ppermute | solution.py:589
  16.1 46.2 %collective-permute-start.1 = (bf16[272,768]{1,0:T(8,128)(2,1)}, bf16[272,768]{1,0:T(8,128)(2,1)S(1)}, u32[]{:S(2)}, u32[]{:S(2)}) collective-permute-start(bf16[272,768]{1,0:T(8,128)(2,1)} %get-tuple-element.49), channel_id=1, source_target_pairs={{0,1},{1,0},{2,5},{3,4},{4,3},{5,2},{6,7},{7,6},{8,9},{9,8},{10,13... | collective-permute-start | bytes 1253384 | tf_op jit(solution)/shard_map/ppermute | solution.py:589
  21.8 20.6 %collective-permute-start.16 = (bf16[64,768]{1,0:T(8,128)(2,1)S(1)}, bf16[64,768]{1,0:T(8,128)(2,1)S(1)}, u32[]{:S(2)}, u32[]{:S(2)}) collective-permute-start(bf16[64,768]{1,0:T(8,128)(2,1)S(1)} %slice.303), channel_id=1, source_target_pairs={{0,3},{1,0},{2,1},{3,2},{4,7},{5,4},{6,5},{7,6},{8,11},{9,8},{10,9... | collective-permute-start | bytes 294920 | tf_op jit(solution)/shard_map/ppermute | solution.py:589
  24.7 19.1 %collective-permute-start.15 = (bf16[64,768]{1,0:T(8,128)(2,1)S(1)}, bf16[64,768]{1,0:T(8,128)(2,1)S(1)}, u32[]{:S(2)}, u32[]{:S(2)}) collective-permute-start(bf16[64,768]{1,0:T(8,128)(2,1)S(1)} %slice.302), channel_id=1, source_target_pairs={{0,1},{1,2},{2,3},{3,0},{4,5},{5,6},{6,7},{7,4},{8,9},{9,10},{10,1... | collective-permute-start | bytes 294920 | tf_op jit(solution)/shard_map/ppermute | solution.py:589
  59.9 13.3 %collective-permute-start.21 = (bf16[2,24,3072]{2,1,0:T(8,128)(2,1)}, bf16[2,24,3072]{2,1,0:T(8,128)(2,1)}, u32[]{:S(2)}, u32[]{:S(2)}) collective-permute-start(bf16[2,24,3072]{2,1,0:T(8,128)(2,1)} %slice.310), channel_id=1, source_target_pairs={{0,8},{1,9},{2,10},{3,11},{4,12},{5,13},{6,14},{7,15},{8,0},{9,1},... | collective-permute-start | bytes 884744 | tf_op jit(solution)/shard_map/ppermute | solution.py:589
  62.2 28.9 %collective-permute-start.17 = (bf16[4,64,768]{2,1,0:T(8,128)(2,1)S(1)}, bf16[4,64,768]{2,1,0:T(8,128)(2,1)}, u32[]{:S(2)}, u32[]{:S(2)}) collective-permute-start(bf16[4,64,768]{2,1,0:T(8,128)(2,1)S(1)} %get-tuple-element.64), channel_id=1, source_target_pairs={{0,16},{1,17},{2,18},{3,19},{4,20},{5,21},{6,22},{7,23},{8,24},{9,... | collective-permute-start | bytes 1179656 | tf_op jit(solution)/shard_map/ppermute | solution.py:589
  63.8 30.3 %collective-permute-start.27 = (bf16[4,64,768]{2,1,0:T(8,128)(2,1)S(1)}, bf16[4,64,768]{2,1,0:T(8,128)(2,1)}, u32[]{:S(2)}, u32[]{:S(2)}) collective-permute-start(bf16[4,64,768]{2,1,0:T(8,128)(2,1)S(1)} %get-tuple-element.63), channel_id=1, source_target_pairs={{0,8},{1,9},{2,10},{3,11},{4,12},{5,13},{6,14},{7,15},{8,0},{9,1},... | collective-permute-start | bytes 1179656 | tf_op jit(solution)/shard_map/ppermute | solution.py:589
  85.4 37.0 %collective-permute-start.2 = (bf16[2,272,768]{2,1,0:T(8,128)(2,1)S(1)}, bf16[2,272,768]{2,1,0:T(8,128)(2,1)S(1)}, u32[]{:S(2)}, u32[]{:S(2)}) collective-permute-start(bf16[2,272,768]{2,1,0:T(8,128)(2,1)S(1)} %broadcast_select_fusion.8), channel_id=1, source_target_pairs={{0,4},{1,5},{2,6},{3,7},{4,0},{5,1},{6,2},{7,3},{8,12},{9,13},{10,... | collective-permute-start | bytes 2506760 | tf_op jit(solution)/shard_map/ppermute | solution.py:589
  103.3 15.3 %collective-permute-start.22 = (bf16[2,2,24,3072]{3,2,1,0:T(8,128)(2,1)S(1)}, bf16[2,2,24,3072]{3,2,1,0:T(8,128)(2,1)S(1)}, u32[]{:S(2)}, u32[]{:S(2)}) collective-permute-start(bf16[2,2,24,3072]{3,2,1,0:T(8,128)(2,1)S(1)} %broadcast_select_fusion.14), channel_id=1, source_target_pairs={{0,16},{1,17},{2,18},{3,19},{4,20},{5,21},{6,22},{7,23},{8,24},{9,... | collective-permute-start | bytes 1769480 | tf_op jit(solution)/shard_map/ppermute | solution.py:589
  106.7 69.8 %collective-permute-start.18 = (bf16[2,4,64,768]{3,2,1,0:T(8,128)(2,1)}, bf16[2,4,64,768]{3,2,1,0:T(8,128)(2,1)}, u32[]{:S(2)}, u32[]{:S(2)}) collective-permute-start(bf16[2,4,64,768]{3,2,1,0:T(8,128)(2,1)} %broadcast_select_fusion.10), channel_id=1, source_target_pairs={{0,8},{1,9},{2,10},{3,11},{4,12},{5,13},{6,14},{7,15},{8,0},{9,1},... | collective-permute-start | bytes 2359304 | tf_op jit(solution)/shard_map/ppermute | solution.py:589
  118.5 60.0 %collective-permute-start.28 = (bf16[2,4,64,768]{3,2,1,0:T(8,128)(2,1)}, bf16[2,4,64,768]{3,2,1,0:T(8,128)(2,1)}, u32[]{:S(2)}, u32[]{:S(2)}) collective-permute-start(bf16[2,4,64,768]{3,2,1,0:T(8,128)(2,1)} %broadcast_select_fusion.9), channel_id=1, source_target_pairs={{0,16},{1,17},{2,18},{3,19},{4,20},{5,21},{6,22},{7,23},{8,24},{9,... | collective-permute-start | bytes 2359304 | tf_op jit(solution)/shard_map/ppermute | solution.py:589
  124.5 66.8 %collective-permute-start.23 = (bf16[8,24,3072]{2,1,0:T(8,128)(2,1)}, bf16[8,24,3072]{2,1,0:T(8,128)(2,1)}, u32[]{:S(2)}, u32[]{:S(2)}) collective-permute-start(bf16[8,24,3072]{2,1,0:T(8,128)(2,1)} %bitcast_select_fusion.2), channel_id=1, source_target_pairs={{0,3},{1,0},{2,1},{3,2},{4,7},{5,4},{6,5},{7,6},{8,11},{9,8},{10,9... | collective-permute-start | bytes 3538952 | tf_op jit(solution)/shard_map/ppermute | solution.py:589
  182.3 31.5 %collective-permute-start.24 = (bf16[8,24,3072]{2,1,0:T(8,128)(2,1)}, bf16[8,24,3072]{2,1,0:T(8,128)(2,1)}, u32[]{:S(2)}, u32[]{:S(2)}) collective-permute-start(bf16[8,24,3072]{2,1,0:T(8,128)(2,1)} %bitcast_select_fusion.2), channel_id=1, source_target_pairs={{0,1},{1,2},{2,3},{3,0},{4,5},{5,6},{6,7},{7,4},{8,9},{9,10},{10,1... | collective-permute-start | bytes 3538952 | tf_op jit(solution)/shard_map/ppermute | solution.py:589
  191.2 50.4 %collective-permute-start.20 = (bf16[512,768]{1,0:T(8,128)(2,1)S(1)}, bf16[512,768]{1,0:T(8,128)(2,1)S(1)}, u32[]{:S(2)}, u32[]{:S(2)}) collective-permute-start(bf16[512,768]{1,0:T(8,128)(2,1)S(1)} %fusion.43), channel_id=1, source_target_pairs={{0,4},{1,5},{2,6},{3,7},{4,0},{5,1},{6,2},{7,3},{8,12},{9,13},{10,... | collective-permute-start | bytes 2359304 | tf_op jit(solution)/shard_map/ppermute | solution.py:589
  192.4 33.9 %collective-permute-start.26 = (bf16[4,24,3072]{2,1,0:T(8,128)(2,1)S(1)}, bf16[4,24,3072]{2,1,0:T(8,128)(2,1)S(1)}, u32[]{:S(2)}, u32[]{:S(2)}) collective-permute-start(bf16[4,24,3072]{2,1,0:T(8,128)(2,1)S(1)} %slice.312), channel_id=1, source_target_pairs={{0,3},{1,0},{2,1},{3,2},{4,7},{5,4},{6,5},{7,6},{8,11},{9,8},{10,9... | collective-permute-start | bytes 1769480 | tf_op jit(solution)/shard_map/ppermute | solution.py:589
  214.9 23.2 %collective-permute-start.25 = (bf16[4,24,3072]{2,1,0:T(8,128)(2,1)S(1)}, bf16[4,24,3072]{2,1,0:T(8,128)(2,1)S(1)}, u32[]{:S(2)}, u32[]{:S(2)}) collective-permute-start(bf16[4,24,3072]{2,1,0:T(8,128)(2,1)S(1)} %slice.311), channel_id=1, source_target_pairs={{0,1},{1,2},{2,3},{3,0},{4,5},{5,6},{6,7},{7,4},{8,9},{9,10},{10,1... | collective-permute-start | bytes 1769480 | tf_op jit(solution)/shard_map/ppermute | solution.py:589
  274.6 172.1 %collective-permute-start.31 = (bf16[256,768]{1,0:T(8,128)(2,1)}, bf16[256,768]{1,0:T(8,128)(2,1)}, u32[]{:S(2)}, u32[]{:S(2)}) collective-permute-start(bf16[256,768]{1,0:T(8,128)(2,1)} %get-tuple-element.60), channel_id=1, source_target_pairs={{0,1},{1,0},{2,5},{3,4},{4,3},{5,2},{6,7},{7,6},{8,9},{9,8},{10,13... | collective-permute-start | bytes 1179656 | tf_op jit(solution)/shard_map/ppermute | solution.py:589
  274.6 172.1 %collective-permute-start.30 = (bf16[256,768]{1,0:T(8,128)(2,1)}, bf16[256,768]{1,0:T(8,128)(2,1)}, u32[]{:S(2)}, u32[]{:S(2)}) collective-permute-start(bf16[256,768]{1,0:T(8,128)(2,1)} %get-tuple-element.59), channel_id=1, source_target_pairs={{0,0},{1,1},{2,4},{3,5},{4,2},{5,3},{6,6},{7,7},{8,8},{9,9},{10,12... | collective-permute-start | bytes 1179656 | tf_op jit(solution)/shard_map/ppermute | solution.py:589
  293.0 50.0 %collective-permute-start.35 = (bf16[512,768]{1,0:T(8,128)(2,1)S(1)}, bf16[512,768]{1,0:T(8,128)(2,1)S(1)}, u32[]{:S(2)}, u32[]{:S(2)}) collective-permute-start(bf16[512,768]{1,0:T(8,128)(2,1)S(1)} %fusion.37), channel_id=1, source_target_pairs={{0,4},{1,5},{2,6},{3,7},{4,0},{5,1},{6,2},{7,3},{8,12},{9,13},{10,... | collective-permute-start | bytes 2359304 | tf_op jit(solution)/shard_map/ppermute | solution.py:589
  308.1 18.1 %collective-permute-start.58 = (bf16[4,24,3072]{2,1,0:T(8,128)(2,1)S(1)}, bf16[4,24,3072]{2,1,0:T(8,128)(2,1)S(1)}, u32[]{:S(2)}, u32[]{:S(2)}) collective-permute-start(bf16[4,24,3072]{2,1,0:T(8,128)(2,1)S(1)} %get-tuple-element.42), channel_id=1, source_target_pairs={{0,1},{1,2},{2,3},{3,0},{4,5},{5,6},{6,7},{7,4},{8,9},{9,10},{10,1... | collective-permute-start | bytes 1769480 | tf_op jit(solution)/shard_map/ppermute | solution.py:589
  310.2 27.8 %collective-permute-start.60 = (bf16[4,24,3072]{2,1,0:T(8,128)(2,1)S(1)}, bf16[4,24,3072]{2,1,0:T(8,128)(2,1)S(1)}, u32[]{:S(2)}, u32[]{:S(2)}) collective-permute-start(bf16[4,24,3072]{2,1,0:T(8,128)(2,1)S(1)} %get-tuple-element.44), channel_id=1, source_target_pairs={{0,3},{1,0},{2,1},{3,2},{4,7},{5,4},{6,5},{7,6},{8,11},{9,8},{10,9... | collective-permute-start | bytes 1769480 | tf_op jit(solution)/shard_map/ppermute | solution.py:589
  326.3 31.0 %collective-permute-start.49 = (bf16[2,4,64,768]{3,2,1,0:T(8,128)(2,1)}, bf16[2,4,64,768]{3,2,1,0:T(8,128)(2,1)}, u32[]{:S(2)}, u32[]{:S(2)}) collective-permute-start(bf16[2,4,64,768]{3,2,1,0:T(8,128)(2,1)} %dynamic-slice_bitcast_fusion.2), channel_id=1, source_target_pairs={{0,8},{1,9},{2,10},{3,11},{4,12},{5,13},{6,14},{7,15},{8,0},{9,1},... | collective-permute-start | bytes 2359304 | tf_op jit(solution)/shard_map/ppermute | solution.py:589
  339.6 74.2 %collective-permute-start.61 = (bf16[8,24,3072]{2,1,0:T(8,128)(2,1)}, bf16[8,24,3072]{2,1,0:T(8,128)(2,1)}, u32[]{:S(2)}, u32[]{:S(2)}) collective-permute-start(bf16[8,24,3072]{2,1,0:T(8,128)(2,1)} %pad_maximum_fusion.3), channel_id=1, source_target_pairs={{0,3},{1,0},{2,1},{3,2},{4,7},{5,4},{6,5},{7,6},{8,11},{9,8},{10,9... | collective-permute-start | bytes 3538952 | tf_op jit(solution)/shard_map/ppermute | solution.py:589
  343.0 72.5 %collective-permute-start.59 = (bf16[8,24,3072]{2,1,0:T(8,128)(2,1)}, bf16[8,24,3072]{2,1,0:T(8,128)(2,1)}, u32[]{:S(2)}, u32[]{:S(2)}) collective-permute-start(bf16[8,24,3072]{2,1,0:T(8,128)(2,1)} %pad_maximum_fusion.2), channel_id=1, source_target_pairs={{0,1},{1,2},{2,3},{3,0},{4,5},{5,6},{6,7},{7,4},{8,9},{9,10},{10,1... | collective-permute-start | bytes 3538952 | tf_op jit(solution)/shard_map/ppermute | solution.py:589
  360.6 29.7 %collective-permute-start.50 = (bf16[4,64,768]{2,1,0:T(8,128)(2,1)}, bf16[4,64,768]{2,1,0:T(8,128)(2,1)}, u32[]{:S(2)}, u32[]{:S(2)}) collective-permute-start(bf16[4,64,768]{2,1,0:T(8,128)(2,1)} %dynamic-slice_bitcast_fusion.13), channel_id=1, source_target_pairs={{0,16},{1,17},{2,18},{3,19},{4,20},{5,21},{6,22},{7,23},{8,24},{9,... | collective-permute-start | bytes 1179656 | tf_op jit(solution)/shard_map/ppermute | solution.py:589
  413.7 20.0 %collective-permute-start.37 = (bf16[512,768]{1,0:T(8,128)(2,1)S(1)}, bf16[512,768]{1,0:T(8,128)(2,1)S(1)}, u32[]{:S(2)}, u32[]{:S(2)}) collective-permute-start(bf16[512,768]{1,0:T(8,128)(2,1)S(1)} %convolution_convert_fusion.4), channel_id=1, source_target_pairs={{0,4},{1,5},{2,6},{3,7},{4,0},{5,1},{6,2},{7,3},{8,12},{9,13},{10,... | collective-permute-start | bytes 2359304 | tf_op jit(solution)/shard_map/ppermute | solution.py:589
  435.9 13.3 %collective-permute-start.39 = (bf16[256,768]{1,0:T(8,128)(2,1)}, bf16[256,768]{1,0:T(8,128)(2,1)}, u32[]{:S(2)}, u32[]{:S(2)}) collective-permute-start(bf16[256,768]{1,0:T(8,128)(2,1)} %get-tuple-element.54), channel_id=1, source_target_pairs={{0,1},{1,0},{2,5},{3,4},{4,3},{5,2},{6,7},{7,6},{8,9},{9,8},{10,13... | collective-permute-start | bytes 1179656 | tf_op jit(solution)/shard_map/ppermute | solution.py:589
  435.9 13.3 %collective-permute-start.38 = (bf16[256,768]{1,0:T(8,128)(2,1)}, bf16[256,768]{1,0:T(8,128)(2,1)}, u32[]{:S(2)}, u32[]{:S(2)}) collective-permute-start(bf16[256,768]{1,0:T(8,128)(2,1)} %get-tuple-element.53), channel_id=1, source_target_pairs={{0,0},{1,1},{2,4},{3,5},{4,2},{5,3},{6,6},{7,7},{8,8},{9,9},{10,12... | collective-permute-start | bytes 1179656 | tf_op jit(solution)/shard_map/ppermute | solution.py:589
  444.7 19.3 %collective-permute-start.62 = (bf16[2,2,24,3072]{3,2,1,0:T(8,128)(2,1)}, bf16[2,2,24,3072]{3,2,1,0:T(8,128)(2,1)}, u32[]{:S(2)}, u32[]{:S(2)}) collective-permute-start(bf16[2,2,24,3072]{3,2,1,0:T(8,128)(2,1)} %fusion.66), channel_id=1, source_target_pairs={{0,16},{1,17},{2,18},{3,19},{4,20},{5,21},{6,22},{7,23},{8,24},{9,... | collective-permute-start | bytes 1769480 | tf_op jit(solution)/shard_map/ppermute | solution.py:589
  468.8 20.7 %collective-permute-start.52 = (bf16[2,4,64,768]{3,2,1,0:T(8,128)(2,1)}, bf16[2,4,64,768]{3,2,1,0:T(8,128)(2,1)}, u32[]{:S(2)}, u32[]{:S(2)}) collective-permute-start(bf16[2,4,64,768]{3,2,1,0:T(8,128)(2,1)} %fusion.60), channel_id=1, source_target_pairs={{0,16},{1,17},{2,18},{3,19},{4,20},{5,21},{6,22},{7,23},{8,24},{9,... | collective-permute-start | bytes 2359304 | tf_op jit(solution)/shard_map/ppermute | solution.py:589
  (96 other events, 841.4 us)

commit v2 on v0

--- a/solution.py
+++ b/solution.py
@@ -3,6 +3,8 @@
 import jax
 import jax.numpy as jnp
 from jax import lax
+from jax.experimental import pallas as pl
+from jax.experimental.pallas import tpu as pltpu
 from jax.sharding import PartitionSpec as P
 
 D = 768
@@ -349,6 +351,718 @@
     )
 
 
+PAIR = 2 * HEAD_DIM
+HALF_D = D // 2
+LOG2E = 1.4426950408889634
+BF = jnp.bfloat16
+F32 = jnp.float32
+AXES = ("dp", "ctx")
+LIGHT = pl.CostEstimate(flops=1024, bytes_accessed=1024, transcendentals=0)
+SIDE, DEPTH = 2, 4
+OWNERS = 2 * SIDE * SIDE * DEPTH
+D_ROWS, FF_ROWS = D // OWNERS, FF // OWNERS
+FF_HALF = FF // 2
+FF_COLS = FF_HALF // (SIDE * SIDE)
+NORM_COLS = 128
+OUT_COLS = HALF_D + NORM_COLS
+Q_COLS = 3 * HALF_D
+NEAR_COLS = Q_COLS + OUT_COLS
+
+
+def dot_nn(left, right):
+    return lax.dot_general(left, right, (((1,), (0,)), ((), ())), preferred_element_type=F32)
+
+
+def dot_nt(left, right):
+    return lax.dot_general(left, right, (((1,), (1,)), ((), ())), preferred_element_type=F32)
+
+
+def dot_tn(left, right):
+    return lax.dot_general(left, right, (((0,), (0,)), ((), ())), preferred_element_type=F32)
+
+
+def swap_halves(tile):
+    lane = lax.broadcasted_iota(jnp.int32, tile.shape, 1)
+    low_half = lax.rem(lane, HEAD_DIM) < HEAD_DIM // 2
+    ahead = pltpu.roll(tile, PAIR - HEAD_DIM // 2, 1)
+    behind = pltpu.roll(tile, HEAD_DIM // 2, 1)
+    return jnp.where(low_half, ahead, behind)
+
+
+def qkv_body(x_ref, w_ref, cos_ref, sin_ref, o_ref):
+    product = dot_nn(x_ref[...], w_ref[...])
+    part = pl.program_id(0)
+
+    @pl.when(part < 2)
+    def _():
+        for c in range(HALF_D // PAIR):
+            tile = product[:, c * PAIR : (c + 1) * PAIR]
+            turned = tile * cos_ref[...] + swap_halves(tile) * sin_ref[...]
+            o_ref[:, c * PAIR : (c + 1) * PAIR] = turned.astype(BF)
+
+    @pl.when(part == 2)
+    def _():
+        o_ref[...] = product.astype(BF)
+
+
+def project_qkv(tokens, weight, cosine, sine):
+    rows = tokens.shape[0]
+    tile = rows
+    return pl.pallas_call(
+        qkv_body,
+        out_shape=jax.ShapeDtypeStruct((rows, 3 * HALF_D), BF),
+        grid=(3, rows // tile),
+        in_specs=[
+            pl.BlockSpec((tile, D), lambda i, r: (r, 0)),
+            pl.BlockSpec((D, HALF_D), lambda i, r: (0, i)),
+            pl.BlockSpec((tile, PAIR), lambda i, r: (r, 0)),
+            pl.BlockSpec((tile, PAIR), lambda i, r: (r, 0)),
+        ],
+        out_specs=pl.BlockSpec((tile, HALF_D), lambda i, r: (r, i)),
+        cost_estimate=LIGHT,
+        compiler_params=pltpu.CompilerParams(vmem_limit_bytes=32 * 2**20),
+        name="project_qkv",
+    )(tokens, weight, cosine, sine)
+
+
+Q_TILE = 256
+
+
+def lane_head(shape):
+    return lax.broadcasted_iota(jnp.int32, shape, 1) // HEAD_DIM
+
+
+def row_head(shape):
+    return lax.broadcasted_iota(jnp.int32, shape, 0) // HEAD_DIM
+
+
+def attend_body(q_ref, k_ref, v_ref, segc_ref, segr_ref, o_ref, l_ref):
+    keys = k_ref[...]
+    values_t = v_ref[...].astype(F32).T.astype(BF)
+    heads_down = row_head(values_t.shape)
+    masked_values = [jnp.where(heads_down == h, values_t, jnp.zeros_like(values_t)) for h in range(2)]
+    rows = q_ref.shape[0]
+    scale = 0.125 * LOG2E
+    for t in range(rows // Q_TILE):
+        span = pl.ds(t * Q_TILE, Q_TILE)
+        queries = q_ref[span, :]
+        heads_across = lane_head(queries.shape)
+        same = segc_ref[...] == segr_ref[:, span]
+        total = jnp.zeros((PAIR, Q_TILE), F32)
+        for h in range(2):
+            scores = dot_nt(keys, jnp.where(heads_across == h, queries, jnp.zeros_like(queries)))
+            scores = jnp.where(same, scores * scale, masked_score)
+            highest = jnp.max(scores, axis=0, keepdims=True)
+            weights = jnp.exp2(scores - highest)
+            norm = jnp.sum(weights, axis=0, keepdims=True)
+            l_ref[h : h + 1, span] = highest + jnp.log2(norm)
+            total = total + dot_nn(masked_values[h], weights.astype(BF)) * (1.0 / norm)
+        o_ref[span, :] = total.T.astype(BF)
+
+
+def attend_pair(pair, qkv, seg_col, seg_row):
+    rows = qkv.shape[0]
+    pairs = HALF_D // PAIR
+    return pl.pallas_call(
+        attend_body,
+        out_shape=(
+            jax.ShapeDtypeStruct((rows, PAIR), BF),
+            jax.ShapeDtypeStruct((8, rows), F32),
+        ),
+        grid=(1,),
+        in_specs=[
+            pl.BlockSpec((rows, PAIR), lambda i: (0, pair)),
+            pl.BlockSpec((rows, PAIR), lambda i: (0, pairs + pair)),
+            pl.BlockSpec((rows, PAIR), lambda i: (0, 2 * pairs + pair)),
+            pl.BlockSpec((rows, 1), lambda i: (0, 0)),
+            pl.BlockSpec((1, rows), lambda i: (0, 0)),
+        ],
+        out_specs=(
+            pl.BlockSpec((rows, PAIR), lambda i: (0, 0)),
+            pl.BlockSpec((8, rows), lambda i: (0, 0)),
+        ),
+        compiler_params=pltpu.CompilerParams(vmem_limit_bytes=40 * 2**20),
+        cost_estimate=LIGHT,
+        name="attend_pair",
+    )(qkv, qkv, qkv, seg_col, seg_row)
+
+
+def attend_back_body(
+    q_ref, k_ref, v_ref, g_ref, l_ref, segc_ref, segr_ref, cos_ref, sin_ref, *others
+):
+    d_ref, dk_sum, dv_sum = others[-3:]
+    keys = k_ref[...]
+    values = v_ref[...]
+    keys_t = keys.astype(F32).T.astype(BF)
+    heads_down = row_head(keys_t.shape)
+    masked_keys = [jnp.where(heads_down == h, keys_t, jnp.zeros_like(keys_t)) for h in range(2)]
+    rows = q_ref.shape[0]
+    scale = 0.125 * LOG2E
+    for t in range(rows // Q_TILE):
+        span = pl.ds(t * Q_TILE, Q_TILE)
+        queries = q_ref[span, :]
+        grads = g_ref[span, :]
+        heads_across = lane_head(queries.shape)
+        same = segc_ref[...] == segr_ref[:, span]
+        dq_t = jnp.zeros((PAIR, Q_TILE), F32)
+        dk_part = None
+        dv_part = None
+        for h in range(2):
+            own_q = jnp.where(heads_across == h, queries, jnp.zeros_like(queries))
+            own_g = jnp.where(heads_across == h, grads, jnp.zeros_like(grads))
+            scores = dot_nt(keys, own_q)
+            logits = jnp.where(same, scores * scale, masked_score)
+            probs = jnp.exp2(logits - l_ref[h : h + 1, span])
+            prob_grad = dot_nt(values, own_g)
+            mixed = probs * prob_grad
+            mean = jnp.sum(mixed, axis=0, keepdims=True)
+            score_grad = (mixed - probs * mean).astype(BF)
+            dv_new = dot_nn(probs.astype(BF), own_g)
+            dk_new = dot_nn(score_grad, own_q)
+            dv_part = dv_new if dv_part is None else dv_part + dv_new
+            dk_part = dk_new if dk_part is None else dk_part + dk_new
+            dq_t = dq_t + dot_nn(masked_keys[h], score_grad)
+        if t == 0:
+            dk_sum[...] = dk_part
+            dv_sum[...] = dv_part
+        else:
+            dk_sum[...] += dk_part
+            dv_sum[...] += dv_part
+        dq = dq_t.T * 0.125
+        d_ref[0, span, :] = (dq * cos_ref[span, :] - swap_halves(dq) * sin_ref[span, :]).astype(BF)
+    dk = dk_sum[...] * 0.125
+    d_ref[1] = (dk * cos_ref[...] - swap_halves(dk) * sin_ref[...]).astype(BF)
+    d_ref[2] = dv_sum[...].astype(BF)
+
+
+def attend_back_pair(pair, earlier, qkv, grads, totals, seg_col, seg_row, cosine, sine):
+    rows = qkv.shape[0]
+    pairs = HALF_D // PAIR
+    column = pl.BlockSpec((rows, PAIR), lambda i: (0, pair))
+    whole = pl.BlockSpec((rows, PAIR), lambda i: (0, 0))
+    carried = [] if earlier is None else [earlier]
+    return pl.pallas_call(
+        attend_back_body,
+        out_shape=jax.ShapeDtypeStruct((3, rows, HALF_D), BF),
+        grid=(1,),
+        in_specs=[
+            column,
+            pl.BlockSpec((rows, PAIR), lambda i: (0, pairs + pair)),
+            pl.BlockSpec((rows, PAIR), lambda i: (0, 2 * pairs + pair)),
+            column,
+            pl.BlockSpec((8, rows), lambda i: (0, 0)),
+            pl.BlockSpec((rows, 1), lambda i: (0, 0)),
+            pl.BlockSpec((1, rows), lambda i: (0, 0)),
+            whole,
+            whole,
+        ] + [pl.BlockSpec(memory_space=pl.ANY)] * len(carried),
+        out_specs=pl.BlockSpec((3, rows, PAIR), lambda i: (0, 0, pair)),
+        scratch_shapes=[pltpu.VMEM((rows, PAIR), F32), pltpu.VMEM((rows, PAIR), F32)],
+        input_output_aliases={9: 0} if carried else {},
+        compiler_params=pltpu.CompilerParams(vmem_limit_bytes=44 * 2**20),
+        cost_estimate=LIGHT,
+        name="attend_back_pair",
+    )(qkv, qkv, qkv, grads, totals, seg_col, seg_row, cosine, sine, *carried)
+
+
+def near_part_body(x_ref, g_ref, s_ref, o_ref):
+    for n in range(3):
+        o_ref[:, n * HALF_D : (n + 1) * HALF_D] = dot_tn(x_ref[...], g_ref[n]).astype(BF)
+    o_ref[:, 3 * HALF_D :] = s_ref[...]
+
+
+def near_weight_part(tokens, grads, out_sum):
+    rows = tokens.shape[0]
+    return pl.pallas_call(
+        near_part_body,
+        out_shape=jax.ShapeDtypeStruct((D, NEAR_COLS), BF),
+        compiler_params=pltpu.CompilerParams(vmem_limit_bytes=32 * 2**20),
+        cost_estimate=LIGHT,
+        name="near_weight_part",
+    )(tokens, grads, out_sum)
+
+
+def row_sum_body(x_ref, g_ref, o_ref):
+    o_ref[...] = dot_tn(x_ref[...], g_ref[...]).astype(BF)
+
+
+def gate_up_weight_part(normed, grads):
+    rows, tile = normed.shape[0], 512
+    return pl.pallas_call(
+        row_sum_body,
+        out_shape=jax.ShapeDtypeStruct((D, FF), BF),
+        grid=(FF // tile,),
+        in_specs=[
+            pl.BlockSpec((rows, D), lambda i: (0, 0)),
+            pl.BlockSpec((rows, tile), lambda i: (0, i)),
+        ],
+        out_specs=pl.BlockSpec((D, tile), lambda i: (0, i)),
+        compiler_params=pltpu.CompilerParams(vmem_limit_bytes=24 * 2**20),
+        cost_estimate=LIGHT,
+        name="gate_up_weight_part",
+    )(normed, grads)
+
+
+def down_weight_part(hidden, grads):
+    rows, tile = hidden.shape[0], 512
+    return pl.pallas_call(
+        row_sum_body,
+        out_shape=jax.ShapeDtypeStruct((FF_HALF, D), BF),
+        grid=(FF_HALF // tile,),
+        in_specs=[
+            pl.BlockSpec((rows, tile), lambda i: (0, i)),
+            pl.BlockSpec((rows, D), lambda i: (0, 0)),
+        ],
+        out_specs=pl.BlockSpec((tile, D), lambda i: (i, 0)),
+        compiler_params=pltpu.CompilerParams(vmem_limit_bytes=24 * 2**20),
+        cost_estimate=LIGHT,
+        name="down_weight_part",
+    )(hidden, grads)
+
+
+def input_part_body(g_ref, w_ref, o_ref):
+    total = dot_nt(g_ref[0], w_ref[:, :HALF_D])
+    for n in range(1, 3):
+        total = total + dot_nt(g_ref[n], w_ref[:, n * HALF_D : (n + 1) * HALF_D])
+    o_ref[...] = total.astype(o_ref.dtype)
+
+
+def input_part(grads, weight, block, dtype):
+    rows = grads.shape[1] // 2
+    return pl.pallas_call(
+        input_part_body,
+        out_shape=jax.ShapeDtypeStruct((rows, D), dtype),
+        grid=(1,),
+        in_specs=[
+            pl.BlockSpec((3, rows, HALF_D), lambda i: (0, block, 0)),
+            pl.BlockSpec((D, 3 * HALF_D), lambda i: (0, 0)),
+        ],
+        out_specs=pl.BlockSpec((rows, D), lambda i: (0, 0)),
+        compiler_params=pltpu.CompilerParams(vmem_limit_bytes=24 * 2**20),
+        cost_estimate=LIGHT,
+        name="input_part",
+    )(grads, weight)
+
+
+def at(array, index, axis=0):
+    return lax.dynamic_index_in_dim(array, index, axis, keepdims=False)
+
+
+def after(value, earlier):
+    return lax.optimization_barrier((value, earlier))[0]
+
+
+def coordinates():
+    place = lax.axis_index("dp")
+    return place // (2 * SIDE), (place // 2) & 1, place & 1, lax.axis_index("ctx")
+
+
+def place(pieces, shapes, moves):
+    dtype = pieces[0].dtype
+    count = len(moves(0, 0, 0, 0))
+    inputs = len(pieces)
+
+    def body(*refs):
+        sources, results, sems = refs[:inputs], refs[inputs:-1], refs[-1]
+        copies = []
+        for n, (piece, part, result, spot) in enumerate(moves(*coordinates())):
+            source = sources[piece] if part is None else sources[piece].at[part]
+            copies.append(pltpu.make_async_copy(source, results[result].at[spot], sems.at[n]))
+        for copy in copies:
+            copy.start()
+        for copy in copies:
+            copy.wait()
+
+    anywhere = pl.BlockSpec(memory_space=pl.ANY)
+    size = sum(math.prod(shape) for shape in shapes) * 2 * jnp.dtype(dtype).itemsize
+    return pl.pallas_call(
+        body,
+        out_shape=tuple(jax.ShapeDtypeStruct(shape, dtype) for shape in shapes),
+        in_specs=[anywhere] * inputs,
+        out_specs=tuple(pl.BlockSpec(memory_space=pltpu.VMEM) for _ in shapes),
+        scratch_shapes=[pltpu.SemaphoreType.DMA((count,))],
+        compiler_params=pltpu.CompilerParams(vmem_limit_bytes=max(8 * 2**20, 2 * size)),
+        cost_estimate=LIGHT,
+        name="place",
+    )(*pieces)
+
+
+def move(array, target):
+    pairs = []
+    for y in range(SIDE):
+        for x in range(SIDE):
+            for k in range(2):
+                for z in range(DEPTH):
+                    ty, tx, tk, tz = target(y, x, k, z)
+                    source = ((y * SIDE + x) * 2 + k) * DEPTH + z
+                    goal = ((ty * SIDE + tx) * 2 + tk) * DEPTH + tz % DEPTH
+                    pairs.append((source, goal))
+    return lax.ppermute(array, AXES, pairs)
+
+
+def core(array):
+    return move(array, lambda y, x, k, z: (y, x, 1 - k, z))
+
+
+def across_x(array):
+    return move(array, lambda y, x, k, z: (y, 1 - x, k, z))
+
+
+def across_y(array):
+    return move(array, lambda y, x, k, z: (1 - y, x, k, z))
+
+
+def up(array):
+    return move(array, lambda y, x, k, z: (y, x, k, z + 1))
+
+
+def down(array):
+    return move(array, lambda y, x, k, z: (y, x, k, z - 1))
+
+
+def order(index, own, other, axis=0):
+    first = jnp.where(index == 0, own, other)
+    second = jnp.where(index == 0, other, own)
+    return jnp.stack([first, second], axis)
+
+
+def ring_near(array):
+    return down(array), up(array)
+
+
+def ring_far(above, below):
+    half = above.shape[0] // 2
+    return up(below[:half]), down(above[half:])
+
+
+def pair_x(array, got):
+    return place(
+        (array, got), [(SIDE, *array.shape)], lambda y, x, k, z: [(n, None, 0, (x ^ n,)) for n in range(2)]
+    )[0]
+
+
+def pair_y(array, got):
+    return place(
+        (array, got), [(SIDE, *array.shape)], lambda y, x, k, z: [(n, None, 0, (y ^ n,)) for n in range(2)]
+    )[0]
+
+
+def spread_z(block, pieces):
+    both = range(2)
+    return place(
+        (block, *pieces),
+        [(DEPTH, *block.shape[1:])] * 2,
+        lambda y, x, k, z: [
+            (n, (m,), m, ((z + step) & 3,)) for n, step in ((0, 0), (1, 1), (2, 3)) for m in both
+        ] + [(3 + m, (0,), m, ((z + 2) & 3,)) for m in both],
+    )
+
+
+def scatter(array, index, across, axis=0):
+    got = across(at(array, 1 - index, axis).astype(BF))
+    return at(array, index, axis).astype(F32) + got.astype(F32)
+
+
+def scatter_far(array, z, axis):
+    far = at(array, (z + 2) & 3, axis).astype(BF)
+    half = far.shape[0] // 2
+    return up(far[:half]), down(far[half:])
+
+
+def scatter_near(array, z, axis, first, second):
+    above, below = at(array, (z + 1) & 3, axis), at(array, (z + 3) & 3, axis)
+    half = above.shape[0] // 2
+    sum_above = (above[:half].astype(F32) + first.astype(F32)).astype(BF)
+    sum_below = (below[half:].astype(F32) + second.astype(F32)).astype(BF)
+    got_a = up(jnp.concatenate([sum_above, above[half:].astype(BF)], 0))
+    got_b = down(jnp.concatenate([below[:half].astype(BF), sum_below], 0))
+    return got_a, got_b
+
+
+def scatter_own(array, z, axis, got_a, got_b):
+    return at(array, z, axis).astype(F32) + got_a.astype(F32) + got_b.astype(F32)
+
+
+def sequence_step(r):
+    return lambda y, x, k, z: (y, x, z // 2, 2 * k + ((r + z) & 1))
+
+
+def to_sequence(blocks, z):
+    return [move(at(blocks, (z + r) & 1), sequence_step(r)) for r in range(2)]
+
+
+def from_sequence(quarters):
+    return [move(quarters[r], sequence_step(r)) for r in range(2)]
+
+
+def chip_local(
+    tokens,
+    segments,
+    positions,
+    qkv_weight,
+    out_weight,
+    gate_up_weight,
+    down_weight,
+    first_gain,
+    first_bias,
+    second_gain,
+    second_bias,
+    output_grad,
+):
+    y, x, k, z = coordinates()
+    quarter = tokens.shape[1]
+    rows = DEPTH * quarter
+    half = rows // 2
+    planes = SIDE * SIDE
+
+    norms = jnp.stack([first_gain, first_bias, second_gain, second_bias], axis=1)
+    norms = jnp.pad(norms, ((0, 0), (0, NORM_COLS - 4)))
+    qkv_own = qkv_weight.reshape(D_ROWS, 3 * D)
+    gate_up_own = gate_up_weight.reshape(D_ROWS, 2 * FF)
+    out_own = out_weight.reshape(D_ROWS, D)
+
+    def column_half(index):
+        def part(matrix, start, width):
+            left, right = matrix[:, start : start + width], matrix[:, start + width : start + 2 * width]
+            return jnp.where(index == 0, left, right)
+
+        pieces = [part(qkv_own, n * D, HALF_D) for n in range(3)]
+        pieces += [part(out_own, 0, HALF_D), norms]
+        pieces += [part(gate_up_own, n * 2 * FF_COLS, FF_COLS) for n in range(2 * planes)]
+        return jnp.concatenate(pieces, axis=1)
+
+    mine, theirs = column_half(k), core(column_half(1 - k))
+    both, every = range(2), slice(None)
+    near_span, gate_up_span = pl.ds(0, NEAR_COLS), pl.ds(NEAR_COLS, FF)
+    near_block, gate_up_block = place(
+        (mine, theirs),
+        [(2, D_ROWS, NEAR_COLS), (2, D_ROWS, FF)],
+        lambda y, x, k, z: [
+            (n, (every, span), r, (k ^ n,)) for n in both for r, span in enumerate((near_span, gate_up_span))
+        ],
+    )
+
+    near_close = ring_near(near_block)
+    near_ring = (*near_close, *ring_far(*near_close))
+    near_a, near_b = spread_z(near_block, near_ring)
+    down_block = after(down_weight.reshape(FF_ROWS, D), near_block)
+    down_x = pair_x(down_block, across_x(down_block))
+    down_y = pair_y(down_x, across_y(down_x)).reshape(planes, FF_ROWS, D)
+
+    extra = jnp.stack([segments, positions >> 5, positions & 31], axis=1).astype(BF)
+    extra = jnp.pad(extra, ((0, 0), (0, 13), (0, D - quarter)))
+    packed = jnp.concatenate([tokens, extra], axis=1)
+    own_tokens = jnp.concatenate(to_sequence(packed, z), axis=0)
+    near_ax = pair_x(near_a, across_x(near_a))
+    near_by = pair_y(near_b, across_y(near_b))
+    gate_up_close = ring_near(after(gate_up_block, (own_tokens, near_ring)))
+    gate_up_far = ring_far(*after(gate_up_close, (near_ax, near_by)))
+    gate_up_ring = (*gate_up_close, *gate_up_far)
+
+    other_tokens = core(after(own_tokens, near_ring))
+    blocks = jnp.concatenate([own_tokens, other_tokens], 0).reshape(DEPTH, quarter + 16, D)
+    all_tokens = blocks[:, :quarter].reshape(rows, D)
+    all_extra = blocks[:, quarter:, :quarter].astype(F32)
+    seg_all = all_extra[:, 0].reshape(rows)
+    pos_all = (all_extra[:, 1] * 32.0 + all_extra[:, 2]).reshape(rows)
+    lane = jnp.arange(PAIR)
+    counter = (lane & (HEAD_DIM // 2 - 1)).astype(F32)
+    inverse = jnp.exp(counter * (-2.0 * math.log(rotary_base) / HEAD_DIM))
+    angles = pos_all[:, None] * inverse
+    cosine = jnp.cos(angles)
+    sine = jnp.where((lane & (HEAD_DIM - 1)) < HEAD_DIM // 2, -1.0, 1.0) * jnp.sin(angles)
+    seg_col, seg_row = seg_all[:, None], seg_all[None, :]
+
+    qkv_mat, out_half = place(
+        (near_ax, across_y(near_ax), near_by, across_x(near_by)),
+        [(SIDE, SIDE, 2, DEPTH, D_ROWS, Q_COLS), (SIDE, SIDE, 2, DEPTH, D_ROWS, OUT_COLS)],
+        lambda y, x, k, z: [
+            (n, (row, every, every, cols), r, ((y ^ n) ^ (k * r), row, 0))
+            for n in both for row in both for r, cols in ((0, pl.ds(0, Q_COLS)), (1, pl.ds(Q_COLS, OUT_COLS)))
+        ] + [
+            (2 + n, (row, every, every, cols), r, (row ^ (k * r), x ^ n, 1))
+            for n in both for row in both for r, cols in ((0, pl.ds(0, Q_COLS)), (1, pl.ds(Q_COLS, OUT_COLS)))
+        ],
+    )
+    qkv_mat, out_half = qkv_mat.reshape(D, Q_COLS), out_half.reshape(D, OUT_COLS)
+    out_other = core(out_half)
+    swapped = jnp.concatenate([out_other[HALF_D:, :HALF_D], out_other[:HALF_D, :HALF_D]], axis=0)
+    own_cols = out_half[:, :HALF_D]
+    out_mat = jnp.concatenate(
+        [jnp.where(k == 0, own_cols, swapped), jnp.where(k == 0, swapped, own_cols)], axis=1
+    )
+    norm_cols = out_half[:, HALF_D : HALF_D + 8].astype(F32)
+    norm_cols = jnp.where(k == 0, norm_cols, jnp.roll(norm_cols, HALF_D, axis=0)).T
+    gain_one, bias_one, gain_two, bias_two = (norm_cols[n] for n in range(4))
+
+    gate_up_a, gate_up_b = after(spread_z(gate_up_block, gate_up_ring), qkv_mat)
+    gate_up_ax = pair_x(gate_up_a, across_x(gate_up_a))
+    gate_up_by = pair_y(gate_up_b, across_y(gate_up_b))
+    down_close = ring_near(after(down_y, gate_up_far))
+
+    token_half = all_tokens[:half].astype(F32)
+    qkv = project_qkv(all_tokens, qkv_mat, cosine, sine)
+    pairs = range(HALF_D // PAIR)
+    attended, totals = [], []
+    for pair in pairs:
+        one, total = attend_pair(pair, qkv, seg_col, seg_row)
+        attended.append(one)
+        totals.append(total)
+    gate_up_ax, gate_up_by = after((gate_up_ax, gate_up_by), attended[1])
+    gate_up_mat = place(
+        (gate_up_ax, across_y(gate_up_ax), gate_up_by, across_x(gate_up_by)),
+        [(SIDE, SIDE, 2, DEPTH, D_ROWS, FF)],
+        lambda y, x, k, z: [
+            (n, (row,), 0, (y ^ n, row, 0)) for n in both for row in both
+        ] + [(2 + n, (row,), 0, (row, x ^ n, 1)) for n in both for row in both],
+    )[0].reshape(D, FF)
+    down_ring = (*down_close, *ring_far(*after(down_close, attended[1])))
+    first, second = pl.ds(0, planes // 2), pl.ds(planes // 2, planes // 2)
+    down_mat = place(
+        (down_y, *down_ring),
+        [(planes, DEPTH, FF_ROWS, D)],
+        lambda y, x, k, z: [
+            (0, None, 0, (every, z)),
+            (1, None, 0, (every, (z + 1) & 3)),
+            (2, None, 0, (every, (z + 3) & 3)),
+            (3, None, 0, (first, (z + 2) & 3)),
+            (4, None, 0, (second, (z + 2) & 3)),
+        ],
+    )[0].reshape(FF_HALF, D)
+    attended = jnp.concatenate(attended, axis=1)
+    attended_rows = jnp.concatenate([attended[:half], core(attended[half:])], axis=1)
+    branch = dot_nn(attended_rows, out_mat)
+    normed_one, hat_one, recip_one = layer_norm(token_half + branch, gain_one, bias_one)
+    normed_own = normed_one.astype(BF)
+    normed_low = jnp.concatenate([normed_own, core(normed_own)], axis=0)
+    grad_quarters = to_sequence(after(output_grad, down_mat), z)
+    gate_up = dot_nn(normed_low, gate_up_mat)
+    gate_part, up_part = gate_up[:, :FF_HALF], gate_up[:, FF_HALF:]
+    sigmoid_gate = jax.nn.sigmoid(gate_part)
+    silu_gate = gate_part * sigmoid_gate
+    hidden = (silu_gate * up_part).astype(BF)
+
+    def sum_cores(left, right):
+        got = core(right(left[half:]).astype(BF))
+        return right(left[:half]) + got.astype(F32)
+
+    mlp_out = sum_cores(hidden, lambda part: dot_nn(part, down_mat))
+    result, hat_two, recip_two = layer_norm(normed_one + mlp_out, gain_two, bias_two)
+    result = result.astype(BF)
+    output_got = from_sequence([result[:quarter], result[quarter:]])
+
+    grad_half = jnp.concatenate(grad_quarters, axis=0).astype(F32)
+    second_grad, second_gain_part, second_bias_part = norm_back(
+        grad_half, hat_two, recip_two, gain_two
+    )
+    mlp_own = second_grad.astype(BF)
+    mlp_grad = jnp.concatenate([mlp_own, core(mlp_own)], axis=0)
+    hidden_grad = dot_nt(mlp_grad, down_mat)
+    gate_grad = hidden_grad * up_part * (sigmoid_gate * (1.0 + gate_part * (1.0 - sigmoid_gate)))
+    up_grad = hidden_grad * silu_gate
+    gate_up_grad = jnp.concatenate([gate_grad, up_grad], axis=1).astype(BF)
+    down_part = down_weight_part(hidden, mlp_grad)
+    gate_up_part = gate_up_weight_part(normed_low, gate_up_grad)
+    normed_grad = second_grad + sum_cores(gate_up_grad, lambda part: dot_nt(part, gate_up_mat))
+    first_grad, first_gain_part, first_bias_part = norm_back(
+        normed_grad, hat_one, recip_one, gain_one
+    )
+    branch_grad = first_grad.astype(BF)
+    attended_own = dot_nt(branch_grad, out_mat).astype(BF)
+    attended_grad = jnp.concatenate(
+        [attended_own[:, :HALF_D], core(attended_own[:, HALF_D:])], axis=0
+    )
+
+    output_got = after(output_got, gate_up_part)
+    output = order(z & 1, output_got[0], output_got[1])
+    down_part = down_part.reshape(planes, DEPTH, FF_ROWS, D)
+    down_far = scatter_far(down_part, z, 1)
+    gate_up_part = gate_up_part.reshape(SIDE, SIDE, 2, DEPTH, D_ROWS, FF)
+    part_a = scatter(gate_up_part[:, :, 0], x, across_x, 1)
+    part_b = scatter(gate_up_part[:, :, 1], y, across_y, 0)
+    down_near = scatter_near(down_part, z, 1, *down_far)
+    down_z = scatter_own(down_part, z, 1, *down_near)
+    attended_grad, part_a, part_b, down_z = lax.optimization_barrier(
+        (attended_grad, part_a, part_b, down_z)
+    )
+    down_y = scatter(down_z.reshape(SIDE, SIDE, FF_ROWS, D), y, across_y)
+    part_a = scatter(part_a, y, across_y)
+    part_b = scatter(part_b, x, across_x)
+
+    out_part = dot_tn(attended_rows, branch_grad)
+    own_rows, other_rows = out_part[:HALF_D], out_part[HALF_D:]
+    out_part = jnp.concatenate(
+        [jnp.where(k == 0, own_rows, other_rows), jnp.where(k == 0, other_rows, own_rows)], axis=0
+    )
+    norm_part = jnp.stack([first_gain_part, first_bias_part, second_gain_part, second_bias_part])
+    norm_part = jnp.pad(norm_part.T, ((0, 0), (0, NORM_COLS - 4)))
+    left_cols, right_cols = out_part[:, :HALF_D], out_part[:, HALF_D:]
+    keep = jnp.concatenate([jnp.where(k == 0, left_cols, right_cols), norm_part], axis=1)
+    give = jnp.concatenate([jnp.where(k == 0, right_cols, left_cols), norm_part], axis=1)
+    out_sum = (keep + core(give.astype(BF)).astype(F32)).astype(BF)
+
+    projected_grad = None
+    for pair in pairs:
+        if pair == 1:
+            attended_grad, down_y = lax.optimization_barrier((attended_grad, down_y))
+        if pair == 2:
+            attended_grad, part_a, part_b = lax.optimization_barrier((attended_grad, part_a, part_b))
+        projected_grad = attend_back_pair(
+            pair, projected_grad, qkv, attended_grad, totals[pair], seg_col, seg_row, cosine, sine
+        )
+    down_share = scatter(down_y, x, across_x).reshape(-1)
+    gate_up_half = jnp.concatenate([part_a, part_b], axis=1)
+    gate_up_far = scatter_far(gate_up_half, z, 0)
+    near_part = near_weight_part(all_tokens, projected_grad, out_sum)
+    near_part = near_part.reshape(SIDE, SIDE, 2, DEPTH, D_ROWS, NEAR_COLS)
+    near_a = scatter(near_part[:, :, 0], x, across_x, 1)
+    near_b = scatter(near_part[:, :, 1], y, across_y, 0)
+    gate_up_near = scatter_near(gate_up_half, z, 0, *gate_up_far)
+    near_a = scatter(near_a, y, across_y)
+    near_b = scatter(near_b, x, across_x)
+    near_half = jnp.concatenate([near_a, near_b], axis=1)
+    near_sum = scatter_own(
+        near_half, z, 0, *scatter_near(near_half, z, 0, *scatter_far(near_half, z, 0))
+    ).reshape(2, D_ROWS, NEAR_COLS)
+    gate_up_sum = scatter_own(gate_up_half, z, 0, *gate_up_near).reshape(2, D_ROWS, FF)
+    gate_up_got = core(at(gate_up_sum, 1 - k).astype(BF)).astype(F32)
+    gate_up_share = order(
+        k,
+        at(gate_up_sum, k).reshape(D_ROWS, 2 * planes, FF_COLS),
+        gate_up_got.reshape(D_ROWS, 2 * planes, FF_COLS),
+        2,
+    ).reshape(-1)
+    near_mine = at(near_sum, k)
+    near_got = core(at(near_sum, 1 - k)[:, : Q_COLS + HALF_D].astype(BF)).astype(F32)
+    qkv_share = order(
+        k,
+        near_mine[:, :Q_COLS].reshape(D_ROWS, 3, HALF_D),
+        near_got[:, :Q_COLS].reshape(D_ROWS, 3, HALF_D),
+        2,
+    ).reshape(-1)
+    out_share = order(k, near_mine[:, Q_COLS : Q_COLS + HALF_D], near_got[:, Q_COLS:], 1).reshape(-1)
+    norm_share = near_mine[:, Q_COLS + HALF_D : Q_COLS + HALF_D + 4].T
+
+    projected_grad = after(projected_grad, near_part)
+    input_got = core(input_part(projected_grad, qkv_mat, 1, BF))
+    input_half = first_grad + input_part(projected_grad, qkv_mat, 0, F32) + input_got.astype(F32)
+    input_half = input_half.astype(BF)
+    input_grad = from_sequence([input_half[:quarter], input_half[quarter:]])
+    input_grad = order(z & 1, input_grad[0], input_grad[1]).astype(F32)
+    return (
+        output,
+        input_grad,
+        qkv_share,
+        out_share,
+        gate_up_share,
+        down_share,
+        norm_share[0],
+        norm_share[1],
+        norm_share[2],
+        norm_share[3],
+    )
+
+
 def solution(mesh):
     in_specs = (
         P("dp", "ctx", None),
@@ -376,4 +1090,6 @@
         P(("dp", "ctx")),
         P(("dp", "ctx")),
     )
-    return jax.shard_map(local, mesh=mesh, in_specs=in_specs, out_specs=out_specs, check_vma=False)
+    fits = mesh.shape["dp"] == 8 and mesh.shape["ctx"] == 4
+    body = chip_local if fits else local
+    return jax.shard_map(body, mesh=mesh, in_specs=in_specs, out_specs=out_specs, check_vma=False)

time: 1350 us -> 392 us (0.29)
  waiting for transfers between devices: 858 us -> 102 us
  matrix products: 194 us -> 25.4 us
  local copies, waits for them, and re-layouts: 158 us -> 44.6 us
  starting transfers between devices: 0.35 us -> 92.4 us
  blocking collectives: 91.1 us -> 0 us
  Pallas kernels: 0 us -> 70.1 us
  other arithmetic: 22 us -> 47.3 us
    unnamed x10 -> x0, waiting for transfers between devices: 505 us -> none
    all_gather x6 -> x0, waiting for transfers between devices: 274 us -> none  [the longest x1 64.2 us: local(): lax.all_gather(qkv_weight, ('dp', 'ctx'), axis=0, tiled=True)]
    dot_general x54 -> x9, matrix products: 194 us -> 25.4 us  [the longest x4 15.7 us: dot_nt(): lax.dot_general(left, right, (((1,), (1,)), ((), ())), preferred_element_...]
    ppermute x0 -> x65, waiting for transfers between devices: none -> 102 us  [move(): return lax.ppermute(array, AXES, pairs)]
    ppermute x0 -> x65, starting transfers between devices: none -> 92.4 us  [move(): return lax.ppermute(array, AXES, pairs)]
    unnamed x2 -> x0, blocking collectives: 81.7 us -> none
    reduce_scatter x2 -> x0, waiting for transfers between devices: 78.7 us -> none  [the longest x1 61.2 us: local(): lax.psum_scatter(key_partial.astype(jnp.bfloat16), 'ctx', scatter_dimensi...]
    pallas_call x0 -> x24, Pallas kernels: none -> 70.1 us  [the longest x3 21 us: attend_back_pair(): pl.pallas_call(attend_back_body, out_shape=jax.ShapeDtypeStruct((3, rows,...]
  transfers between devices with their start and end apart: 9 -> 65, of which waited for: 8 -> 30; matrix products, arithmetic and copies ran while one was open for 9% -> 23% of each run, Pallas kernels for 0% -> 18%
where the time goes in v2:
time: 392 us; the launch traced here: 385 us
  waiting for transfers between devices  102 us (26%)
  starting transfers between devices  92.4 us (24%)
  Pallas kernels  70.1 us (18%)
  other arithmetic  47.3 us (12%)
  local copies, waits for them, and re-layouts  44.6 us (11%)
  matrix products  25.4 us (6%)
    ppermute x65, waiting for transfers between devices, move(): return lax.ppermute(array, AXES, pairs)  102 us
    ppermute x65, starting transfers between devices, move(): return lax.ppermute(array, AXES, pairs)  92.4 us
    pallas_call x3, Pallas kernels, attend_back_pair(): pl.pallas_call(attend_back_body, out_shape=jax.ShapeDtypeStruct((3, rows,...  21 us
    pallas_call x3, Pallas kernels, attend_pair(): pl.pallas_call(attend_body, out_shape=(jax.ShapeDtypeStruct((rows, PAIR),...  18.2 us
    unnamed x174, local copies, waits for them, and re-layouts  16.4 us
    dot_general x4, matrix products, dot_nt(): lax.dot_general(left, right, (((1,), (1,)), ((), ())), preferred_element_...  15.7 us
    add x10, other arithmetic, scatter(): return at(array, index, axis).astype(F32) + got.astype(F32)  10.5 us
    pallas_call x12, Pallas kernels, place(): pl.pallas_call(body, out_shape=tuple((jax.ShapeDtypeStruct(shape, dtype)...  9.7 us
  transfers between devices with their start and end apart: 65, of which 30 were waited for; matrix products, arithmetic and copies ran while one was open for 23% of the time, Pallas kernels for 18%

profile of v2, /device:TPU:0, one launch (start us, length us, event | category | flops | bytes accessed | tf_op | source)
XLA Modules:
  0.0 384.9 jit_solution(1529561121409795081)
XLA Ops:
  4.4 5.4 %collective-permute-start.2 = (bf16[24,4736]{1,0:T(8,128)(2,1)S(1)}, bf16[24,4736]{1,0:T(8,128)(2,1)S(1)}, u32[]{:S(2)}, u32[]{:S(2)}) collective-permute-start(bf16[24,4736]{1,0:T(8,128)(2,1)S(1)} %get-tuple-element.155), channel_id=1, source_target_pairs={{0,4},{1,5},{2,6},{3,7},{4,0},{5,1},{6,2},{7,3},{8,12},{9,13},{10,... | collective-permute-start | bytes 681992 | tf_op jit(solution)/shard_map/ppermute | solution.py:700
  15.5 14.5 %collective-permute-done.4.refs_2_ = bf16[2,24,1664]{2,1,0:T(8,128)(2,1)S(1)} collective-permute-done((bf16[2,24,1664]{2,1,0:T(8,128)(2,1)S(1)}, bf16[2,24,1664]{2,1,0:T(8,128)(2,1)S(1)}, u32[]{:S(2)}, u32[]{:S(2)}) %collective-permute-start.4) | collective-permute-done | bytes 159776 | tf_op jit(solution)/shard_map/ppermute | solution.py:700
  55.5 5.4 %collective-permute-done.16.refs_2_ = bf16[2,24,3072]{2,1,0:T(8,128)(2,1)S(1)} collective-permute-done((bf16[2,24,3072]{2,1,0:T(8,128)(2,1)S(1)}, bf16[2,24,3072]{2,1,0:T(8,128)(2,1)S(1)}, u32[]{:S(2)}, u32[]{:S(2)}) %collective-permute-start.16) | collective-permute-done | bytes 294944 | tf_op jit(solution)/shard_map/ppermute | solution.py:700
  84.1 5.7 %project_qkv.1.q_ref.k_ref.v_ref = bf16[1024,1152]{1,0:T(8,128)(2,1)S(1)} custom-call(bf16[1024,768]{1,0:T(8,128)(2,1)S(1)} %bitcast.210, bf16[768,1152]{1,0:T(8,128)(2,1)S(1)} %bitcast.207, f32[1024,128]{1,0:T(8,128)S(1)} %get-tuple-element.186.cos_ref, f32[1024,128]{1,0:T(8,128)S(1)} %get-tuple-element.185.sin_ref), custom_call_target="tpu_custom_call" | custom-call | flops 1024 | bytes 1024 | tf_op jit(solution)/shard_map/project_qkv/pallas_call | solution.py:411
  89.8 6.0 %attend_pair.3 = (bf16[1024,128]{1,0:T(8,128)(2,1)S(1)}, f32[8,1024]{1,0:T(8,128)S(1)}) custom-call(bf16[1024,1152]{1,0:T(8,128)(2,1)S(1)} %project_qkv.1.q_ref.k_ref.v_ref, bf16[1024,1152]{1,0:T(8,128)(2,1)S(1)} %project_qkv.1.q_ref.k_ref.v_ref, bf16[1024,1152]{1,0:T(8,128)(2,1)S(1)} %project_qkv.1.q_ref.k_ref.v_ref, f32[1024,1]{1,0:T(8,128)S(1)} %copy.85.segc_ref, ...), custom_call_target="tpu_custom_call" | custom-call | flops 1024 | bytes 1024 | tf_op jit(solution)/shard_map/attend_pair/pallas_call | solution.py:466
  95.8 6.0 %attend_pair.4 = (bf16[1024,128]{1,0:T(8,128)(2,1)S(1)}, f32[8,1024]{1,0:T(8,128)S(1)}) custom-call(bf16[1024,1152]{1,0:T(8,128)(2,1)S(1)} %project_qkv.1.q_ref.k_ref.v_ref, bf16[1024,1152]{1,0:T(8,128)(2,1)S(1)} %project_qkv.1.q_ref.k_ref.v_ref, bf16[1024,1152]{1,0:T(8,128)(2,1)S(1)} %project_qkv.1.q_ref.k_ref.v_ref, f32[1024,1]{1,0:T(8,128)S(1)} %copy.85.segc_ref, ...), custom_call_target="tpu_custom_call" | custom-call | flops 1024 | bytes 1024 | tf_op jit(solution)/shard_map/attend_pair/pallas_call | solution.py:466
  111.1 6.2 %attend_pair.5 = (bf16[1024,128]{1,0:T(8,128)(2,1)S(1)}, f32[8,1024]{1,0:T(8,128)S(1)}) custom-call(bf16[1024,1152]{1,0:T(8,128)(2,1)S(1)} %project_qkv.1.q_ref.k_ref.v_ref, bf16[1024,1152]{1,0:T(8,128)(2,1)S(1)} %project_qkv.1.q_ref.k_ref.v_ref, bf16[1024,1152]{1,0:T(8,128)(2,1)S(1)} %project_qkv.1.q_ref.k_ref.v_ref, f32[1024,1]{1,0:T(8,128)S(1)} %copy.85.segc_ref, ...), custom_call_target="tpu_custom_call" | custom-call | flops 1024 | bytes 1024 | tf_op jit(solution)/shard_map/attend_pair/pallas_call | solution.py:466
  119.3 4.6 %collective-permute-done.20.refs_1_ = bf16[4,24,3072]{2,1,0:T(8,128)(2,1)S(1)} collective-permute-done((bf16[4,24,3072]{2,1,0:T(8,128)(2,1)}, bf16[4,24,3072]{2,1,0:T(8,128)(2,1)S(1)}, u32[]{:S(2)}, u32[]{:S(2)}) %collective-permute-start.20) | collective-permute-done | bytes 589856 | tf_op jit(solution)/shard_map/ppermute | solution.py:700
  137.4 6.8 %collective-permute-done.27.refs_3_ = bf16[2,96,768]{2,1,0:T(8,128)(2,1)S(1)} collective-permute-done((bf16[2,96,768]{2,1,0:T(8,128)(2,1)S(1)}, bf16[2,96,768]{2,1,0:T(8,128)(2,1)S(1)}, u32[]{:S(2)}, u32[]{:S(2)}) %collective-permute-start.27) | collective-permute-done | bytes 294944 | tf_op jit(solution)/shard_map/ppermute | solution.py:700
  144.2 5.4 %collective-permute-done.28.refs_4_ = bf16[2,96,768]{2,1,0:T(8,128)(2,1)S(1)} collective-permute-done((bf16[2,96,768]{2,1,0:T(8,128)(2,1)S(1)}, bf16[2,96,768]{2,1,0:T(8,128)(2,1)S(1)}, u32[]{:S(2)}, u32[]{:S(2)}) %collective-permute-start.28) | collective-permute-done | bytes 294944 | tf_op jit(solution)/shard_map/ppermute | solution.py:700
  154.3 5.0 %fusion.77 = f32[1024,3072]{1,0:T(8,128)S(1)} fusion(bf16[768,3072]{1,0:T(8,128)(2,1)S(1)} %bitcast.217, bf16[512,768]{1,0:T(8,128)(2,1)S(1)} %collective-permute-done.14, bf16[512,768]{1,0:T(8,128)(2,1)S(1)} %fusion.30), kind=kOutput, calls=%fused_computation.262 | convolution fusion | flops 4834983936 | bytes 18874368 | tf_op jit(solution)/shard_map/dot_general | solution.py:373
  169.7 7.3 %collective-permute-done.33 = bf16[256,768]{1,0:T(8,128)(2,1)S(1)} collective-permute-done((bf16[256,768]{1,0:T(8,128)(2,1)S(1)}, bf16[256,768]{1,0:T(8,128)(2,1)S(1)}, u32[]{:S(2)}, u32[]{:S(2)}) %collective-permute-start.33) | collective-permute-done | bytes 393248 | tf_op jit(solution)/shard_map/ppermute | solution.py:700
  179.6 7.4 %collective-permute-start.34 = (bf16[512,768]{1,0:T(8,128)(2,1)}, bf16[512,768]{1,0:T(8,128)(2,1)}, u32[]{:S(2)}, u32[]{:S(2)}) collective-permute-start(bf16[512,768]{1,0:T(8,128)(2,1)} %get-tuple-element.121), channel_id=1, source_target_pairs={{0,4},{1,5},{2,6},{3,7},{4,0},{5,1},{6,2},{7,3},{8,12},{9,13},{10,... | collective-permute-start | bytes 2359304 | tf_op jit(solution)/shard_map/ppermute | solution.py:700
  190.7 4.5 %collective-permute-start.30 = (bf16[256,768]{1,0:T(8,128)(2,1)}, bf16[256,768]{1,0:T(8,128)(2,1)}, u32[]{:S(2)}, u32[]{:S(2)}) collective-permute-start(bf16[256,768]{1,0:T(8,128)(2,1)} %get-tuple-element.140), channel_id=1, source_target_pairs={{0,0},{1,1},{2,4},{3,5},{4,2},{5,3},{6,6},{7,7},{8,8},{9,9},{10,12... | collective-permute-start | bytes 1179656 | tf_op jit(solution)/shard_map/ppermute | solution.py:700
  195.2 4.8 %collective-permute-start.31 = (bf16[256,768]{1,0:T(8,128)(2,1)}, bf16[256,768]{1,0:T(8,128)(2,1)}, u32[]{:S(2)}, u32[]{:S(2)}) collective-permute-start(bf16[256,768]{1,0:T(8,128)(2,1)} %get-tuple-element.139), channel_id=1, source_target_pairs={{0,1},{1,0},{2,5},{3,4},{4,3},{5,2},{6,7},{7,6},{8,9},{9,8},{10,13... | collective-permute-start | bytes 1179656 | tf_op jit(solution)/shard_map/ppermute | solution.py:700
  200.0 7.8 %multiply_convert_fusion.1 = (bf16[1024,1536]{1,0:T(8,128)(2,1)S(1)}, bf16[1024,1536]{1,0:T(8,128)(2,1)S(1)}) fusion(f32[1024,3072]{1,0:T(8,128)} %copy-done.31, bf16[1536,768]{1,0:T(8,128)(2,1)S(1)} %bitcast.226, bf16[512,768]{1,0:T(8,128)(2,1)} %collective-permute-done.34, bf16[512,768]{1,0:T(8,128)(2,1)} %get-tuple-element.121), kind=kOutput, calls=%fused_computation.6 | convolution fusion | flops 2439512064 | bytes 22806528 | tf_op jit(solution)/shard_map/dot_general | solution.py:377
  207.9 3.5 fusion.24
  214.0 3.7 pad_maximum_fusion.g_ref
  222.9 3.6 collective-permute-start.41
  226.5 6.8 %gate_up_weight_part.1 = bf16[768,3072]{1,0:T(8,128)(2,1)S(1)} custom-call(bf16[1024,768]{1,0:T(8,128)(2,1)S(1)} %copy-done.14, bf16[1024,3072]{1,0:T(8,128)(2,1)S(1)} %pad_maximum_fusion.g_ref), custom_call_target="tpu_custom_call" | custom-call | flops 1024 | bytes 1024 | tf_op jit(solution)/shard_map/gate_up_weight_part/pallas_call | solution.py:591
  242.8 4.0 %collective-permute-start.42 = (bf16[4,96,768]{2,1,0:T(8,128)(2,1)}, bf16[4,96,768]{2,1,0:T(8,128)(2,1)}, u32[]{:S(2)}, u32[]{:S(2)}) collective-permute-start(bf16[4,96,768]{2,1,0:T(8,128)(2,1)} %pad_maximum_fusion.15), channel_id=1, source_target_pairs={{0,3},{1,0},{2,1},{3,2},{4,7},{5,4},{6,5},{7,6},{8,11},{9,8},{10,9... | collective-permute-start | bytes 1769480 | tf_op jit(solution)/shard_map/ppermute | solution.py:700
  246.9 3.5 multiply_reduce_fusion
  260.8 10.9 %collective-permute-done.42 = bf16[4,96,768]{2,1,0:T(8,128)(2,1)} collective-permute-done((bf16[4,96,768]{2,1,0:T(8,128)(2,1)}, bf16[4,96,768]{2,1,0:T(8,128)(2,1)}, u32[]{:S(2)}, u32[]{:S(2)}) %collective-permute-start.42) | collective-permute-done | bytes 589856 | tf_op jit(solution)/shard_map/ppermute | solution.py:700
  282.8 7.3 %attend_back_pair.3.others_0_ = bf16[3,1024,384]{2,1,0:T(8,128)(2,1)S(1)} custom-call(bf16[1024,1152]{1,0:T(8,128)(2,1)S(1)} %project_qkv.1.q_ref.k_ref.v_ref, bf16[1024,1152]{1,0:T(8,128)(2,1)S(1)} %project_qkv.1.q_ref.k_ref.v_ref, bf16[1024,1152]{1,0:T(8,128)(2,1)S(1)} %project_qkv.1.q_ref.k_ref.v_ref, bf16[1024,384]{1,0:T(8,128)(2,1)S(1)} %pad_maximum_fusion.9.g_ref, ...), custom_call_target="tpu_custom_call" | custom-call | flops 1024 | bytes 1024 | tf_op jit(solution)/shard_map/attend_back_pair/pallas_call | solution.py:544
  291.2 6.8 %attend_back_pair.4.others_0_ = bf16[3,1024,384]{2,1,0:T(8,128)(2,1)S(1)} custom-call(bf16[1024,1152]{1,0:T(8,128)(2,1)S(1)} %project_qkv.1.q_ref.k_ref.v_ref, bf16[1024,1152]{1,0:T(8,128)(2,1)S(1)} %project_qkv.1.q_ref.k_ref.v_ref, bf16[1024,1152]{1,0:T(8,128)(2,1)S(1)} %project_qkv.1.q_ref.k_ref.v_ref, ...), custom_call_target="tpu_custom_call", output_to_operand_aliasing={{}: (9, {})} | custom-call | flops 1024 | bytes 1024 | tf_op jit(solution)/shard_map/attend_back_pair/pallas_call | solution.py:544
  307.7 6.8 %attend_back_pair.5.g_ref = bf16[3,1024,384]{2,1,0:T(8,128)(2,1)S(1)} custom-call(bf16[1024,1152]{1,0:T(8,128)(2,1)S(1)} %project_qkv.1.q_ref.k_ref.v_ref, bf16[1024,1152]{1,0:T(8,128)(2,1)S(1)} %project_qkv.1.q_ref.k_ref.v_ref, bf16[1024,1152]{1,0:T(8,128)(2,1)S(1)} %project_qkv.1.q_ref.k_ref.v_ref, ...), custom_call_target="tpu_custom_call", output_to_operand_aliasing={{}: (9, {})} | custom-call | flops 1024 | bytes 1024 | tf_op jit(solution)/shard_map/attend_back_pair/pallas_call | solution.py:544
  320.6 4.5 %collective-permute-start.62 = (bf16[48,3072]{1,0:T(8,128)(2,1)S(1)}, bf16[48,3072]{1,0:T(8,128)(2,1)S(1)}, u32[]{:S(2)}, u32[]{:S(2)}) collective-permute-start(bf16[48,3072]{1,0:T(8,128)(2,1)S(1)} %pad_maximum_fusion.21), channel_id=1, source_target_pairs={{0,3},{1,0},{2,1},{3,2},{4,7},{5,4},{6,5},{7,6},{8,11},{9,8},{10,9... | collective-permute-start | bytes 884744 | tf_op jit(solution)/shard_map/ppermute | solution.py:700
  337.7 4.5 %collective-permute-done.52 = bf16[2,4,24,1664]{3,2,1,0:T(8,128)(2,1)} collective-permute-done((bf16[2,4,24,1664]{3,2,1,0:T(8,128)(2,1)}, bf16[2,4,24,1664]{3,2,1,0:T(8,128)(2,1)}, u32[]{:S(2)}, u32[]{:S(2)}) %collective-permute-start.52) | collective-permute-done | bytes 639008 | tf_op jit(solution)/shard_map/ppermute | solution.py:700
  354.0 3.9 %collective-permute-start.56 = (bf16[24,1664]{1,0:T(8,128)(2,1)S(1)}, bf16[24,1664]{1,0:T(8,128)(2,1)S(1)}, u32[]{:S(2)}, u32[]{:S(2)}) collective-permute-start(bf16[24,1664]{1,0:T(8,128)(2,1)S(1)} %get-tuple-element.172), channel_id=1, source_target_pairs={{0,3},{1,0},{2,1},{3,2},{4,7},{5,4},{6,5},{7,6},{8,11},{9,8},{10,9... | collective-permute-start | bytes 239624 | tf_op jit(solution)/shard_map/ppermute | solution.py:700
  357.8 7.1 %collective-permute-done.54 = bf16[24,1664]{1,0:T(8,128)(2,1)S(1)} collective-permute-done((bf16[24,1664]{1,0:T(8,128)(2,1)S(1)}, bf16[24,1664]{1,0:T(8,128)(2,1)S(1)}, u32[]{:S(2)}, u32[]{:S(2)}) %collective-permute-start.54) | collective-permute-done | bytes 79904 | tf_op jit(solution)/shard_map/ppermute | solution.py:700
  365.0 3.5 collective-permute-done.56
  372.8 7.3 %collective-permute-done.57 = bf16[48,1664]{1,0:T(8,128)(2,1)S(1)} collective-permute-done((bf16[48,1664]{1,0:T(8,128)(2,1)S(1)}, bf16[48,1664]{1,0:T(8,128)(2,1)S(1)}, u32[]{:S(2)}, u32[]{:S(2)}) %collective-permute-start.57) | collective-permute-done | bytes 159776 | tf_op jit(solution)/shard_map/ppermute | solution.py:700
  (466 shorter events, 191.3 us)
Async XLA Ops:
  2.8 31.1 %collective-permute-start = (bf16[272,768]{1,0:T(8,128)(2,1)S(1)}, bf16[272,768]{1,0:T(8,128)(2,1)S(1)}, u32[]{:S(2)}, u32[]{:S(2)}) collective-permute-start(bf16[272,768]{1,0:T(8,128)(2,1)S(1)} %get-tuple-element.128), channel_id=1, source_target_pairs={{0,0},{1,1},{2,4},{3,5},{4,2},{5,3},{6,6},{7,7},{8,8},{9,9},{10,12... | collective-permute-start | bytes 1253384 | tf_op jit(solution)/shard_map/ppermute | solution.py:700
  9.8 24.9 %collective-permute-start.1 = (bf16[272,768]{1,0:T(8,128)(2,1)S(1)}, bf16[272,768]{1,0:T(8,128)(2,1)S(1)}, u32[]{:S(2)}, u32[]{:S(2)}) collective-permute-start(bf16[272,768]{1,0:T(8,128)(2,1)S(1)} %get-tuple-element.127), channel_id=1, source_target_pairs={{0,1},{1,0},{2,5},{3,4},{4,3},{5,2},{6,7},{7,6},{8,9},{9,8},{10,13... | collective-permute-start | bytes 1253384 | tf_op jit(solution)/shard_map/ppermute | solution.py:700
  11.6 18.4 %collective-permute-start.4 = (bf16[2,24,1664]{2,1,0:T(8,128)(2,1)S(1)}, bf16[2,24,1664]{2,1,0:T(8,128)(2,1)S(1)}, u32[]{:S(2)}, u32[]{:S(2)}) collective-permute-start(bf16[2,24,1664]{2,1,0:T(8,128)(2,1)S(1)} %get-tuple-element.49.refs_0_), channel_id=1, source_target_pairs={{0,1},{1,2},{2,3},{3,0},{4,5},{5,6},{6,7},{7,4},{8,9},{9,10},{10,1... | collective-permute-start | bytes 479240 | tf_op jit(solution)/shard_map/ppermute | solution.py:700
  12.8 19.3 %collective-permute-start.3 = (bf16[2,24,1664]{2,1,0:T(8,128)(2,1)S(1)}, bf16[2,24,1664]{2,1,0:T(8,128)(2,1)S(1)}, u32[]{:S(2)}, u32[]{:S(2)}) collective-permute-start(bf16[2,24,1664]{2,1,0:T(8,128)(2,1)S(1)} %get-tuple-element.49.refs_0_), channel_id=1, source_target_pairs={{0,3},{1,0},{2,1},{3,2},{4,7},{5,4},{6,5},{7,6},{8,11},{9,8},{10,9... | collective-permute-start | bytes 479240 | tf_op jit(solution)/shard_map/ppermute | solution.py:700
  38.1 37.5 %collective-permute-start.7 = (bf16[544,768]{1,0:T(8,128)(2,1)}, bf16[544,768]{1,0:T(8,128)(2,1)}, u32[]{:S(2)}, u32[]{:S(2)}) collective-permute-start(bf16[544,768]{1,0:T(8,128)(2,1)} %constant_dynamic-update-slice_fusion), channel_id=1, source_target_pairs={{0,4},{1,5},{2,6},{3,7},{4,0},{5,1},{6,2},{7,3},{8,12},{9,13},{10,... | collective-permute-start | bytes 2506760 | tf_op jit(solution)/shard_map/ppermute | solution.py:700
  65.8 15.3 %collective-permute-start.11 = (bf16[2,4,24,1664]{3,2,1,0:T(8,128)(2,1)S(1)}, bf16[2,4,24,1664]{3,2,1,0:T(8,128)(2,1)S(1)}, u32[]{:S(2)}, u32[]{:S(2)}) collective-permute-start(bf16[2,4,24,1664]{3,2,1,0:T(8,128)(2,1)S(1)} %place.15.refs_2_), channel_id=1, source_target_pairs={{0,8},{1,9},{2,10},{3,11},{4,12},{5,13},{6,14},{7,15},{8,0},{9,1},... | collective-permute-start | bytes 1916936 | tf_op jit(solution)/shard_map/ppermute | solution.py:700
  69.5 61.7 %collective-permute-start.25 = (bf16[4,96,768]{2,1,0:T(8,128)(2,1)}, bf16[4,96,768]{2,1,0:T(8,128)(2,1)}, u32[]{:S(2)}, u32[]{:S(2)}) collective-permute-start(bf16[4,96,768]{2,1,0:T(8,128)(2,1)} %bitcast.19.refs_0_), channel_id=1, source_target_pairs={{0,3},{1,0},{2,1},{3,2},{4,7},{5,4},{6,5},{7,6},{8,11},{9,8},{10,9... | collective-permute-start | bytes 1769480 | tf_op jit(solution)/shard_map/ppermute | solution.py:700
  72.3 59.0 %collective-permute-start.26 = (bf16[4,96,768]{2,1,0:T(8,128)(2,1)}, bf16[4,96,768]{2,1,0:T(8,128)(2,1)}, u32[]{:S(2)}, u32[]{:S(2)}) collective-permute-start(bf16[4,96,768]{2,1,0:T(8,128)(2,1)} %bitcast.19.refs_0_), channel_id=1, source_target_pairs={{0,1},{1,2},{2,3},{3,0},{4,5},{5,6},{6,7},{7,4},{8,9},{9,10},{10,1... | collective-permute-start | bytes 1769480 | tf_op jit(solution)/shard_map/ppermute | solution.py:700
  102.5 23.5 %collective-permute-start.13 = (bf16[768,512]{1,0:T(8,128)(2,1)}, bf16[768,512]{1,0:T(8,128)(2,1)}, u32[]{:S(2)}, u32[]{:S(2)}) collective-permute-start(bf16[768,512]{1,0:T(8,128)(2,1)} %bitcast.16), channel_id=1, source_target_pairs={{0,4},{1,5},{2,6},{3,7},{4,0},{5,1},{6,2},{7,3},{8,12},{9,13},{10,... | collective-permute-start | bytes 2359304 | tf_op jit(solution)/shard_map/ppermute | solution.py:700
  108.0 16.0 %collective-permute-start.20 = (bf16[4,24,3072]{2,1,0:T(8,128)(2,1)}, bf16[4,24,3072]{2,1,0:T(8,128)(2,1)S(1)}, u32[]{:S(2)}, u32[]{:S(2)}) collective-permute-start(bf16[4,24,3072]{2,1,0:T(8,128)(2,1)} %copy-done.22), channel_id=1, source_target_pairs={{0,16},{1,17},{2,18},{3,19},{4,20},{5,21},{6,22},{7,23},{8,24},{9,... | collective-permute-start | bytes 1769480 | tf_op jit(solution)/shard_map/ppermute | solution.py:700
  108.5 15.7 %collective-permute-start.19 = (bf16[4,24,3072]{2,1,0:T(8,128)(2,1)}, bf16[4,24,3072]{2,1,0:T(8,128)(2,1)S(1)}, u32[]{:S(2)}, u32[]{:S(2)}) collective-permute-start(bf16[4,24,3072]{2,1,0:T(8,128)(2,1)} %copy-done.20), channel_id=1, source_target_pairs={{0,8},{1,9},{2,10},{3,11},{4,12},{5,13},{6,14},{7,15},{8,0},{9,1},... | collective-permute-start | bytes 1769480 | tf_op jit(solution)/shard_map/ppermute | solution.py:700
  124.5 28.4 %collective-permute-start.21 = (bf16[2,4,24,3072]{3,2,1,0:T(8,128)(2,1)S(1)}, bf16[2,4,24,3072]{3,2,1,0:T(8,128)(2,1)S(1)}, u32[]{:S(2)}, u32[]{:S(2)}) collective-permute-start(bf16[2,4,24,3072]{3,2,1,0:T(8,128)(2,1)S(1)} %place.18.refs_0_), channel_id=1, source_target_pairs={{0,16},{1,17},{2,18},{3,19},{4,20},{5,21},{6,22},{7,23},{8,24},{9,... | collective-permute-start | bytes 3538952 | tf_op jit(solution)/shard_map/ppermute | solution.py:700
  126.0 27.2 %collective-permute-start.22 = (bf16[2,4,24,3072]{3,2,1,0:T(8,128)(2,1)S(1)}, bf16[2,4,24,3072]{3,2,1,0:T(8,128)(2,1)S(1)}, u32[]{:S(2)}, u32[]{:S(2)}) collective-permute-start(bf16[2,4,24,3072]{3,2,1,0:T(8,128)(2,1)S(1)} %place.19.refs_2_), channel_id=1, source_target_pairs={{0,8},{1,9},{2,10},{3,11},{4,12},{5,13},{6,14},{7,15},{8,0},{9,1},... | collective-permute-start | bytes 3538952 | tf_op jit(solution)/shard_map/ppermute | solution.py:700
  131.2 23.1 %collective-permute-start.14 = (bf16[512,768]{1,0:T(8,128)(2,1)S(1)}, bf16[512,768]{1,0:T(8,128)(2,1)S(1)}, u32[]{:S(2)}, u32[]{:S(2)}) collective-permute-start(bf16[512,768]{1,0:T(8,128)(2,1)S(1)} %fusion.30), channel_id=1, source_target_pairs={{0,4},{1,5},{2,6},{3,7},{4,0},{5,1},{6,2},{7,3},{8,12},{9,13},{10,... | collective-permute-start | bytes 2359304 | tf_op jit(solution)/shard_map/ppermute | solution.py:700
  134.3 15.3 %collective-permute-start.28 = (bf16[2,96,768]{2,1,0:T(8,128)(2,1)S(1)}, bf16[2,96,768]{2,1,0:T(8,128)(2,1)S(1)}, u32[]{:S(2)}, u32[]{:S(2)}) collective-permute-start(bf16[2,96,768]{2,1,0:T(8,128)(2,1)S(1)} %slice.411), channel_id=1, source_target_pairs={{0,3},{1,0},{2,1},{3,2},{4,7},{5,4},{6,5},{7,6},{8,11},{9,8},{10,9... | collective-permute-start | bytes 884744 | tf_op jit(solution)/shard_map/ppermute | solution.py:700
  179.6 20.4 %collective-permute-start.34 = (bf16[512,768]{1,0:T(8,128)(2,1)}, bf16[512,768]{1,0:T(8,128)(2,1)}, u32[]{:S(2)}, u32[]{:S(2)}) collective-permute-start(bf16[512,768]{1,0:T(8,128)(2,1)} %get-tuple-element.121), channel_id=1, source_target_pairs={{0,4},{1,5},{2,6},{3,7},{4,0},{5,1},{6,2},{7,3},{8,12},{9,13},{10,... | collective-permute-start | bytes 2359304 | tf_op jit(solution)/shard_map/ppermute | solution.py:700
  190.7 46.8 %collective-permute-start.30 = (bf16[256,768]{1,0:T(8,128)(2,1)}, bf16[256,768]{1,0:T(8,128)(2,1)}, u32[]{:S(2)}, u32[]{:S(2)}) collective-permute-start(bf16[256,768]{1,0:T(8,128)(2,1)} %get-tuple-element.140), channel_id=1, source_target_pairs={{0,0},{1,1},{2,4},{3,5},{4,2},{5,3},{6,6},{7,7},{8,8},{9,9},{10,12... | collective-permute-start | bytes 1179656 | tf_op jit(solution)/shard_map/ppermute | solution.py:700
  195.2 43.4 %collective-permute-start.31 = (bf16[256,768]{1,0:T(8,128)(2,1)}, bf16[256,768]{1,0:T(8,128)(2,1)}, u32[]{:S(2)}, u32[]{:S(2)}) collective-permute-start(bf16[256,768]{1,0:T(8,128)(2,1)} %get-tuple-element.139), channel_id=1, source_target_pairs={{0,1},{1,0},{2,5},{3,4},{4,3},{5,2},{6,7},{7,6},{8,9},{9,8},{10,13... | collective-permute-start | bytes 1179656 | tf_op jit(solution)/shard_map/ppermute | solution.py:700
  222.6 18.1 %collective-permute-start.39 = (bf16[2,96,768]{2,1,0:T(8,128)(2,1)S(1)}, bf16[2,96,768]{2,1,0:T(8,128)(2,1)S(1)}, u32[]{:S(2)}, u32[]{:S(2)}) collective-permute-start(bf16[2,96,768]{2,1,0:T(8,128)(2,1)S(1)} %get-tuple-element.118), channel_id=1, source_target_pairs={{0,1},{1,2},{2,3},{3,0},{4,5},{5,6},{6,7},{7,4},{8,9},{9,10},{10,1... | collective-permute-start | bytes 884744 | tf_op jit(solution)/shard_map/ppermute | solution.py:700
  222.9 17.9 %collective-permute-start.41 = (bf16[2,96,768]{2,1,0:T(8,128)(2,1)S(1)}, bf16[2,96,768]{2,1,0:T(8,128)(2,1)S(1)}, u32[]{:S(2)}, u32[]{:S(2)}) collective-permute-start(bf16[2,96,768]{2,1,0:T(8,128)(2,1)S(1)} %get-tuple-element.120), channel_id=1, source_target_pairs={{0,3},{1,0},{2,1},{3,2},{4,7},{5,4},{6,5},{7,6},{8,11},{9,8},{10,9... | collective-permute-start | bytes 884744 | tf_op jit(solution)/shard_map/ppermute | solution.py:700
  234.9 38.4 %collective-permute-start.38 = (bf16[2,4,24,3072]{3,2,1,0:T(8,128)(2,1)}, bf16[2,4,24,3072]{3,2,1,0:T(8,128)(2,1)}, u32[]{:S(2)}, u32[]{:S(2)}) collective-permute-start(bf16[2,4,24,3072]{3,2,1,0:T(8,128)(2,1)} %dynamic-slice_bitcast_fusion), channel_id=1, source_target_pairs={{0,16},{1,17},{2,18},{3,19},{4,20},{5,21},{6,22},{7,23},{8,24},{9,... | collective-permute-start | bytes 3538952 | tf_op jit(solution)/shard_map/ppermute | solution.py:700
  237.5 37.6 %collective-permute-start.37 = (bf16[2,4,24,3072]{3,2,1,0:T(8,128)(2,1)}, bf16[2,4,24,3072]{3,2,1,0:T(8,128)(2,1)}, u32[]{:S(2)}, u32[]{:S(2)}) collective-permute-start(bf16[2,4,24,3072]{3,2,1,0:T(8,128)(2,1)} %dynamic-slice_bitcast_fusion.1), channel_id=1, source_target_pairs={{0,8},{1,9},{2,10},{3,11},{4,12},{5,13},{6,14},{7,15},{8,0},{9,1},... | collective-permute-start | bytes 3538952 | tf_op jit(solution)/shard_map/ppermute | solution.py:700
  241.9 18.3 %collective-permute-start.40 = (bf16[4,96,768]{2,1,0:T(8,128)(2,1)}, bf16[4,96,768]{2,1,0:T(8,128)(2,1)}, u32[]{:S(2)}, u32[]{:S(2)}) collective-permute-start(bf16[4,96,768]{2,1,0:T(8,128)(2,1)} %pad_maximum_fusion.14), channel_id=1, source_target_pairs={{0,1},{1,2},{2,3},{3,0},{4,5},{5,6},{6,7},{7,4},{8,9},{9,10},{10,1... | collective-permute-start | bytes 1769480 | tf_op jit(solution)/shard_map/ppermute | solution.py:700
  242.8 28.9 %collective-permute-start.42 = (bf16[4,96,768]{2,1,0:T(8,128)(2,1)}, bf16[4,96,768]{2,1,0:T(8,128)(2,1)}, u32[]{:S(2)}, u32[]{:S(2)}) collective-permute-start(bf16[4,96,768]{2,1,0:T(8,128)(2,1)} %pad_maximum_fusion.15), channel_id=1, source_target_pairs={{0,3},{1,0},{2,1},{3,2},{4,7},{5,4},{6,5},{7,6},{8,11},{9,8},{10,9... | collective-permute-start | bytes 1769480 | tf_op jit(solution)/shard_map/ppermute | solution.py:700
  260.0 17.6 %collective-permute-start.36 = (bf16[512,384]{1,0:T(8,128)(2,1)}, bf16[512,384]{1,0:T(8,128)(2,1)S(1)}, u32[]{:S(2)}, u32[]{:S(2)}) collective-permute-start(bf16[512,384]{1,0:T(8,128)(2,1)} %get-tuple-element.134), channel_id=1, source_target_pairs={{0,4},{1,5},{2,6},{3,7},{4,0},{5,1},{6,2},{7,3},{8,12},{9,13},{10,... | collective-permute-start | bytes 1179656 | tf_op jit(solution)/shard_map/ppermute | solution.py:700
  260.2 37.9 %collective-permute-start.46 = (bf16[768,512]{1,0:T(8,128)(2,1)S(1)}, bf16[768,512]{1,0:T(8,128)(2,1)S(1)}, u32[]{:S(2)}, u32[]{:S(2)}) collective-permute-start(bf16[768,512]{1,0:T(8,128)(2,1)S(1)} %pad_maximum_fusion.10), channel_id=1, source_target_pairs={{0,4},{1,5},{2,6},{3,7},{4,0},{5,1},{6,2},{7,3},{8,12},{9,13},{10,... | collective-permute-start | bytes 2359304 | tf_op jit(solution)/shard_map/ppermute | solution.py:700
  280.1 22.1 %collective-permute-start.45 = (bf16[4,24,3072]{2,1,0:T(8,128)(2,1)}, bf16[4,24,3072]{2,1,0:T(8,128)(2,1)}, u32[]{:S(2)}, u32[]{:S(2)}) collective-permute-start(bf16[4,24,3072]{2,1,0:T(8,128)(2,1)} %fusion.35), channel_id=1, source_target_pairs={{0,8},{1,9},{2,10},{3,11},{4,12},{5,13},{6,14},{7,15},{8,0},{9,1},... | collective-permute-start | bytes 1769480 | tf_op jit(solution)/shard_map/ppermute | solution.py:700
  282.0 21.9 %collective-permute-start.44 = (bf16[4,24,3072]{2,1,0:T(8,128)(2,1)}, bf16[4,24,3072]{2,1,0:T(8,128)(2,1)}, u32[]{:S(2)}, u32[]{:S(2)}) collective-permute-start(bf16[4,24,3072]{2,1,0:T(8,128)(2,1)} %fusion.34), channel_id=1, source_target_pairs={{0,16},{1,17},{2,18},{3,19},{4,20},{5,21},{6,22},{7,23},{8,24},{9,... | collective-permute-start | bytes 1769480 | tf_op jit(solution)/shard_map/ppermute | solution.py:700
  332.5 15.4 %collective-permute-start.47 = (bf16[512,768]{1,0:T(8,128)(2,1)S(1)}, bf16[512,768]{1,0:T(8,128)(2,1)}, u32[]{:S(2)}, u32[]{:S(2)}) collective-permute-start(bf16[512,768]{1,0:T(8,128)(2,1)S(1)} %input_part.3), channel_id=1, source_target_pairs={{0,4},{1,5},{2,6},{3,7},{4,0},{5,1},{6,2},{7,3},{8,12},{9,13},{10,... | collective-permute-start | bytes 2359304 | tf_op jit(solution)/shard_map/ppermute | solution.py:700
  349.4 19.5 %collective-permute-start.48 = (bf16[256,768]{1,0:T(8,128)(2,1)S(1)}, bf16[256,768]{1,0:T(8,128)(2,1)S(1)}, u32[]{:S(2)}, u32[]{:S(2)}) collective-permute-start(bf16[256,768]{1,0:T(8,128)(2,1)S(1)} %get-tuple-element.131), channel_id=1, source_target_pairs={{0,0},{1,1},{2,4},{3,5},{4,2},{5,3},{6,6},{7,7},{8,8},{9,9},{10,12... | collective-permute-start | bytes 1179656 | tf_op jit(solution)/shard_map/ppermute | solution.py:700
  350.1 18.8 %collective-permute-start.49 = (bf16[256,768]{1,0:T(8,128)(2,1)S(1)}, bf16[256,768]{1,0:T(8,128)(2,1)S(1)}, u32[]{:S(2)}, u32[]{:S(2)}) collective-permute-start(bf16[256,768]{1,0:T(8,128)(2,1)S(1)} %get-tuple-element.132), channel_id=1, source_target_pairs={{0,1},{1,0},{2,5},{3,4},{4,3},{5,2},{6,7},{7,6},{8,9},{9,8},{10,13... | collective-permute-start | bytes 1179656 | tf_op jit(solution)/shard_map/ppermute | solution.py:700
  354.0 14.5 %collective-permute-start.56 = (bf16[24,1664]{1,0:T(8,128)(2,1)S(1)}, bf16[24,1664]{1,0:T(8,128)(2,1)S(1)}, u32[]{:S(2)}, u32[]{:S(2)}) collective-permute-start(bf16[24,1664]{1,0:T(8,128)(2,1)S(1)} %get-tuple-element.172), channel_id=1, source_target_pairs={{0,3},{1,0},{2,1},{3,2},{4,7},{5,4},{6,5},{7,6},{8,11},{9,8},{10,9... | collective-permute-start | bytes 239624 | tf_op jit(solution)/shard_map/ppermute | solution.py:700
  (116 other events, 833.3 us)
